TPU v7x, 128 devices: a whole 4x4x4 slice. The times are simulated.
128 devices in a mesh: row: 8 (over x, core), col: 16 (over y, z).
Axes of the slice: x: 4, y: 4, z: 4, core: 2. Of those that a mesh axis runs over, the one named last changes fastest.
Arguments:
- samples: float32 [384, 32768], P(None, ('row', 'col')), may hold values from -6 to 6
- omega_tiles: float32 [8, 16, 15, 256, 256], P('row', 'col'), may hold values from -6 to 6
- omega_diag: float32 [32768, 256], P(('row', 'col')), as said below
- tile_rows: int32 [8, 16, 15], P('row', 'col'), may hold values from 0 to 15, as said below
- tile_cols: int32 [8, 16, 15], P('row', 'col'), may hold values from 0 to 7
- tile_active: int32 [8, 16, 15], P('row', 'col'), may hold values from 0 to 1, as said below
Outputs:
- new_tiles: float32 [8, 16, 15, 256, 256], P('row', 'col')
- new_diag: float32 [32768, 256], P(('row', 'col'))
Inputs may be any that keep to these rules, and one draw needn't show every extreme that they name: `tile_rows`: on each device the 15 listed tiles (I, J) are distinct and none is diagonal; with o = (J - I) mod (128), o is odd and below 64, or even and above it, so no tile is listed together with its mirror. `tile_active`: on each device the live slots come first and number at least 5; on device (0, 0) all are live. `omega_diag`: every diagonal tile is symmetric and its diagonal entries lie between 0.5 and 4.
All inputs are finite; a program needn't handle non-finite values.
Results may differ from a plain program's by a relative error of at most 0.0003.
Values sent between devices are 32-bit elements; how exact they have to be, the bound alone decides.
A program may use at most 128 MiB of HBM per device.

v0:
```python
import jax
import jax.numpy as jnp
from jax import lax
from jax.sharding import PartitionSpec as P

HIGHEST = lax.Precision.HIGHEST
STEP_SIZE = 0.05
PENALTY = 4.0


def soft_shrink(values, limit):
    return jnp.sign(values) * jnp.maximum(jnp.abs(values) - limit, 0.0)


def per_device(samples, omega_tiles, omega_diag, tile_rows, tile_cols, tile_active):
    row_count = lax.axis_size("row")
    col_count = lax.axis_size("col")
    row_index = lax.axis_index("row")
    col_index = lax.axis_index("col")
    samp_count, tile_side = samples.shape
    tile_set = omega_tiles[0, 0]
    left_ids = tile_rows[0, 0]
    right_ids = tile_cols[0, 0]
    active = tile_active[0, 0]
    row_panel = lax.all_gather(samples, "col", axis=1, tiled=True).reshape(
        samp_count, col_count, tile_side
    )
    col_panel = lax.all_gather(samples, "row", axis=1, tiled=True).reshape(
        samp_count, row_count, tile_side
    )
    x_left = jnp.take(row_panel, left_ids, axis=1)
    x_right = jnp.take(col_panel, right_ids, axis=1)
    pick_right = (right_ids[:, None] == jnp.arange(row_count, dtype=jnp.int32)[None, :]).astype(
        jnp.float32
    )
    pick_left = (left_ids[:, None] == jnp.arange(col_count, dtype=jnp.int32)[None, :]).astype(
        jnp.float32
    )
    own_right = (jnp.arange(row_count, dtype=jnp.int32) == row_index).astype(jnp.float32)
    y_terms = jnp.einsum("nsk,skl->snl", x_left, tile_set, precision=HIGHEST)
    y_part = jnp.einsum("sb,snl->bnl", pick_right, y_terms, precision=HIGHEST)
    y_part = (
        y_part + own_right[:, None, None] * jnp.dot(samples, omega_diag, precision=HIGHEST)[None]
    )
    w_terms = jnp.einsum("nsl,skl->snk", x_right, tile_set, precision=HIGHEST)
    w_part = jnp.einsum("sa,snk->ank", pick_left, w_terms, precision=HIGHEST)
    y_full = lax.psum(y_part, "row")
    w_full = lax.psum(w_part, "col")
    y_own = lax.dynamic_slice_in_dim(y_full, row_index, 1, 0)
    w_own = lax.dynamic_slice_in_dim(w_full, col_index, 1, 0)
    y_row = lax.all_gather(y_own, "col", axis=0, tiled=True)
    w_col = lax.all_gather(w_own, "row", axis=0, tiled=True)
    z_col = y_full + w_col
    z_row = w_full + y_row
    z_own = (y_own + w_own)[0]
    z_right = jnp.take(z_col, right_ids, axis=0)
    z_left = jnp.take(z_row, left_ids, axis=0)
    gradient = jnp.einsum("nsk,snl->skl", x_left, z_right, precision=HIGHEST)
    gradient = gradient + jnp.einsum("snk,nsl->skl", z_left, x_right, precision=HIGHEST)
    gradient = gradient / (2.0 * samp_count)
    stepped = tile_set - STEP_SIZE * gradient
    updated = jnp.where(
        active[:, None, None] > 0, soft_shrink(stepped, STEP_SIZE * PENALTY), tile_set
    )
    identity = jnp.eye(tile_side, dtype=jnp.float32)
    inverse = 1.0 / jnp.diagonal(omega_diag)
    diag_grad = jnp.dot(samples.T, z_own, precision=HIGHEST) + jnp.dot(
        z_own.T, samples, precision=HIGHEST
    )
    diag_grad = diag_grad / (2.0 * samp_count) - identity * inverse[None, :]
    diag_step = omega_diag - STEP_SIZE * diag_grad
    new_diag = jnp.where(identity > 0, diag_step, soft_shrink(diag_step, STEP_SIZE * PENALTY))
    return (updated[None, None], new_diag)


def solution(mesh):
    in_specs = (
        P(None, ("row", "col")),
        P("row", "col", None, None, None),
        P(("row", "col"), None),
        P("row", "col", None),
        P("row", "col", None),
        P("row", "col", None),
    )
    out_specs = (P("row", "col", None, None, None), P(("row", "col"), None))
    return jax.shard_map(
        per_device, mesh=mesh, in_specs=in_specs, out_specs=out_specs, check_vma=False
    )
```

profile of v0, /device:TPU:1, one launch (start us, length us, event | category | flops | bytes accessed | tf_op | source)
XLA Modules:
  0.0 457.9 jit_solution(9830519394448397970)
XLA Ops:
  11.3 30.2 %all-gather.7.cloned.1.call-done = f32[384,2048]{0,1:T(8,128)} async-done(((f32[384,256]{0,1:T(8,128)}), f32[384,2048]{0,1:T(8,128)}) %all-gather.7.cloned.1.call-update) | async-done | bytes 3145744 | tf_op jit(solution)/shard_map/all_gather | solution.py:28
  41.5 2.4 copy.33
  43.9 3.5 gather_fusion.1
  47.4 11.6 %fusion.6 = f32[15,384,256]{2,1,0:T(8,128)S(1)} fusion(f32[15,384,256]{2,1,0:T(8,128)} %gather_fusion.1, f32[1,1,15,256,256]{4,3,2,1,0:T(8,128)} %param.7, pred[15]{0:T(512)(128)(4,1)S(1)} %compare_and_fusion), kind=kOutput, calls=%fused_computation.12 | convolution fusion | flops 4531322880 | bytes 15728655 | tf_op jit(solution)/shard_map/nsl,skl->snk/dot_general | solution.py:45
  59.1 7.1 %fusion = f32[16,384,256]{2,0,1:T(8,128)} fusion(f32[15,384,256]{2,1,0:T(8,128)S(1)} %fusion.6, s32[15]{0:T(128)S(1)} %bitcast.71), kind=kOutput, calls=%fused_computation.6 | convolution fusion | flops 283115776 | bytes 12189756 | tf_op jit(solution)/shard_map/sa,snk->ank/dot_general | solution.py:46
  67.7 37.3 %all-gather.5.cloned.1.call-done = f32[384,4096]{0,1:T(8,128)} async-done(((f32[384,256]{0,1:T(8,128)}), f32[384,4096]{0,1:T(8,128)}) %all-gather.5.cloned.1.call-update) | async-done | bytes 6291472 | tf_op jit(solution)/shard_map/all_gather | solution.py:25
  105.1 6.6 %copy.30 = f32[384,16,256]{2,0,1:T(8,128)} copy(f32[384,16,256]{0,2,1:T(8,128)} %bitcast.69) | data formatting | bytes 12582912 | tf_op jit(solution)/shard_map/reshape | solution.py:25
  111.7 6.8 %gather_fusion = f32[15,384,256]{2,1,0:T(8,128)} fusion(f32[384,16,256]{2,0,1:T(8,128)} %copy.30, s32[1024]{0:T(1024)S(1)} %pad_clamp_fusion.1), kind=kCustom, calls=%fused_computation | custom fusion | bytes 11796540 | tf_op jit(solution)/shard_map/jit(_take)/gather | solution.py:31
  118.5 9.4 %fusion.10 = f32[15,384,256]{2,1,0:T(8,128)S(1)} fusion(f32[15,384,256]{2,1,0:T(8,128)} %gather_fusion, f32[1,1,15,256,256]{4,3,2,1,0:T(8,128)} %param.7, pred[15]{0:T(512)(128)(4,1)S(1)} %compare_and_fusion.1), kind=kOutput, calls=%fused_computation.16 | convolution fusion | flops 4531322880 | bytes 15728655 | tf_op jit(solution)/shard_map/nsk,skl->snl/dot_general | solution.py:40
  128.0 7.6 %multiply_add_fusion = f32[8,384,256]{2,0,1:T(8,128)} fusion(f32[15,384,256]{2,1,0:T(8,128)S(1)} %fusion.10, f32[384,256]{1,0:T(8,128)S(1)} %fusion.57, f32[8]{0:T(128)S(1)} %compare_convert_fusion, s32[15]{0:T(128)S(1)} %bitcast.72), kind=kOutput, calls=%fused_computation.30 | convolution fusion | flops 143130752 | bytes 9437276 | tf_op jit(solution)/shard_map/sb,snl->bnl/dot_general | solution.py:41
  135.7 94.9 %all-reduce.5.cloned.1.call-done = f32[16,384,256]{2,0,1:T(8,128)} async-done(((f32[16,384,256]{2,0,1:T(8,128)}), f32[16,384,256]{2,0,1:T(8,128)}) %all-reduce.5.cloned.1.call-update) | async-done | bytes 6291472 | tf_op jit(solution)/shard_map/psum | solution.py:48
  230.5 69.8 %all-reduce.3.cloned.1.call-done = f32[8,384,256]{2,0,1:T(8,128)} async-done(((f32[8,384,256]{2,0,1:T(8,128)}), f32[8,384,256]{2,0,1:T(8,128)}) %all-reduce.3.cloned.1.call-update) | async-done | bytes 3145744 | tf_op jit(solution)/shard_map/psum | solution.py:47
  300.4 4.5 fusion.56
  307.6 2.6 gather_fusion.4
  310.2 2.6 fusion.37
  316.6 19.1 %all-gather.9.cloned.1.call-done = f32[8,384,256]{2,1,0:T(8,128)} async-done(((f32[1,384,256]{2,1,0:T(8,128)}), f32[8,384,256]{2,1,0:T(8,128)}) %all-gather.9.cloned.1.call-update) | async-done | bytes 3145744 | tf_op jit(solution)/shard_map/all_gather | solution.py:52
  335.6 3.8 copy_add_fusion.1
  340.4 3.4 gather_fusion.2
  343.8 54.7 %all-gather.11.cloned.1.call-done = f32[16,384,256]{2,1,0:T(8,128)} async-done(((f32[1,384,256]{2,1,0:T(8,128)}), f32[16,384,256]{2,1,0:T(8,128)}) %all-gather.11.cloned.1.call-update) | async-done | bytes 6291472 | tf_op jit(solution)/shard_map/all_gather | solution.py:51
  398.5 8.4 %copy_add_fusion = f32[16,384,256]{2,0,1:T(8,128)S(1)} fusion(f32[16,384,256]{2,0,1:T(8,128)} %all-reduce.5.cloned.1.call-done, f32[16,384,256]{2,1,0:T(8,128)} %all-gather.11.cloned.1.call-done), kind=kLoop, calls=%fused_computation.5 | loop fusion | flops 1572864 | bytes 18874368 | tf_op jit(solution)/shard_map/add | solution.py:54
  406.9 6.7 %copy.41 = f32[16,384,256]{2,1,0:T(8,128)} copy(f32[16,384,256]{2,0,1:T(8,128)S(1)} %copy_add_fusion) | data formatting | bytes 12582912 | tf_op jit(solution)/shard_map/add | solution.py:54
  413.6 6.4 %gather_fusion.3 = f32[15,384,256]{2,1,0:T(8,128)} fusion(f32[16,384,256]{2,1,0:T(8,128)} %copy.41, s32[1024]{0:T(1024)S(1)} %pad_clamp_fusion.1), kind=kCustom, calls=%fused_computation.3 | custom fusion | bytes 11796540 | tf_op jit(solution)/shard_map/jit(_take)/gather | solution.py:57
  420.0 15.0 %fusion.4 = f32[15,256,256]{2,1,0:T(8,128)S(1)} fusion(f32[15,384,256]{2,1,0:T(8,128)} %gather_fusion.3, f32[15,384,256]{2,1,0:T(8,128)} %gather_fusion.1, pred[15]{0:T(512)(128)(4,1)S(1)} %compare_and_fusion.1, pred[15]{0:T(512)(128)(4,1)S(1)} %compare_and_fusion), kind=kOutput, calls=%fused_computation.10 | convolution fusion | flops 4532797440 | bytes 15728670 | tf_op jit(solution)/shard_map/snk,nsl->skl/dot_general | solution.py:59
  435.0 15.8 %fusion.20 = f32[1,1,15,256,256]{4,3,2,1,0:T(8,128)} fusion(f32[1,1,15,256,256]{4,3,2,1,0:T(8,128)S(1)} %copy-done, f32[15,256,256]{2,1,0:T(8,128)S(1)} %fusion.4, pred[15]{0:T(512)(128)(4,1)S(1)} %compare_bitcast_fusion, f32[15,384,256]{2,1,0:T(8,128)} %gather_fusion.2, pred[15]{0:T(512)(128)(4,1)S(1)} %compare_and_fusion, ...), kind=kOutput, calls=%fused_computation.28 | convolution fusion | flops 4541644800 | bytes 23593004 | tf_op jit(solution)/shard_map/nsk,snl->skl/dot_general | solution.py:58
  (48 shorter events, 13.0 us)
Async XLA Ops:
  7.2 34.4 %all-gather.7.cloned.1.call-start = ((), (), s32[]{:S(2)}) async-start(), calls=%async_computation.2 | async-start | bytes 3538944 | tf_op jit(solution)/shard_map/all_gather | solution.py:28
  9.1 95.9 %all-gather.5.cloned.1.call-start = ((), (), s32[]{:S(2)}) async-start(), calls=%async_computation | async-start | bytes 6684672 | tf_op jit(solution)/shard_map/all_gather | solution.py:25
  9.9 220.7 %all-reduce.5.cloned.1.call-start = ((), (), s32[]{:S(2)}) async-start(), calls=%async_computation.3 | async-start | bytes 12582912 | tf_op jit(solution)/shard_map/psum | solution.py:48
  47.4 11.7 %copy-start.4 = (s32[1,1,15]{2,1,0:T(1,128)S(1)}, s32[1,1,15]{2,1,0:T(1,128)}, u32[]{:S(2)}) copy-start(s32[1,1,15]{2,1,0:T(1,128)} %param.9) | copy-start | bytes 184
  66.2 0.9 copy-start.1
  66.2 1.1 copy-start.3
  66.2 234.2 %all-reduce.3.cloned.1.call-start = ((), (), s32[]{:S(2)}) async-start(), calls=%async_computation.1 | async-start | bytes 6291456 | tf_op jit(solution)/shard_map/psum | solution.py:47
  118.5 9.4 %copy-start.5 = (s32[1,1,15]{2,1,0:T(1,128)S(1)}, s32[1,1,15]{2,1,0:T(1,128)}, u32[]{:S(2)}) copy-start(s32[1,1,15]{2,1,0:T(1,128)} %param.10) | copy-start | bytes 184
  135.6 174.6 %copy-start.6 = (s32[1,1,15]{2,1,0:T(1,128)S(1)}, s32[1,1,15]{2,1,0:T(1,128)}, u32[]{:S(2)}) copy-start(s32[1,1,15]{2,1,0:T(1,128)} %param.11) | copy-start | bytes 184
  135.6 200.0 %all-gather.9.cloned.1.call-start = ((), (), s32[]{:S(2)}) async-start(), calls=%async_computation.4 | async-start | bytes 3538944 | tf_op jit(solution)/shard_map/all_gather | solution.py:52
  300.4 35.2 %copy-start.2 = (f32[8,384,256]{2,0,1:T(8,128)S(1)}, f32[8,384,256]{2,0,1:T(8,128)}, u32[]{:S(2)}) copy-start(f32[8,384,256]{2,0,1:T(8,128)} %all-reduce.3.cloned.1.call-done) | copy-start | bytes 9437188
  305.7 92.7 %all-gather.11.cloned.1.call-start = ((), (), s32[]{:S(2)}) async-start(), calls=%async_computation.5 | async-start | bytes 6684672 | tf_op jit(solution)/shard_map/all_gather | solution.py:51
  413.6 21.3 %slice-start = ((s8[5898240]{0:T(1024)(128)(4,1)}), s8[1703936]{0:T(1024)(128)(4,1)S(1)}, s32[]{:S(2)}) async-start(s8[5898240]{0:T(1024)(128)(4,1)} %bitcast.66), calls=%async_computation.6 | async-start | bytes 3407872
  420.0 15.0 %slice-start.1 = ((s8[5898240]{0:T(1024)(128)(4,1)}), s8[4194304]{0:T(1024)(128)(4,1)S(1)}, s32[]{:S(2)}) async-start(s8[5898240]{0:T(1024)(128)(4,1)} %bitcast.66), calls=%async_computation.7 | async-start | bytes 8388608
  420.0 15.0 %copy-start = (f32[1,1,15,256,256]{4,3,2,1,0:T(8,128)S(1)}, f32[1,1,15,256,256]{4,3,2,1,0:T(8,128)}, u32[]{:S(2)}) copy-start(f32[1,1,15,256,256]{4,3,2,1,0:T(8,128)} %param.7) | copy-start | bytes 11796484
Sparse Core Ops, SparseCore 0:
  10.2 31.2 all-gather.6
  44.3 60.7 all-gather.4
  108.5 121.9 all-reduce.4
  233.3 66.9 all-reduce.2
  305.9 29.7 all-gather.8
  337.7 60.7 all-gather.10
where the time goes:
time: 464 us; the launch traced here: 458 us
  waiting for transfers between devices  307 us (66%)
  matrix products  69.7 us (15%)
  local copies, waits for them, and re-layouts  46.5 us (10%)
  other arithmetic  20 us (4%)
  between operations  14.5 us (3%)
    psum x1, waiting for transfers between devices, per_device(): w_full = lax.psum(w_part, 'col')  94.9 us
    psum x1, waiting for transfers between devices, per_device(): y_full = lax.psum(y_part, 'row')  69.8 us
    all_gather x1, waiting for transfers between devices, per_device(): y_row = lax.all_gather(y_own, 'col', axis=0, tiled=True)  54.7 us
    all_gather x1, waiting for transfers between devices, per_device(): lax.all_gather(samples, 'col', axis=1, tiled=True)  37.3 us
    all_gather x1, waiting for transfers between devices, per_device(): lax.all_gather(samples, 'row', axis=1, tiled=True)  30.2 us
    all_gather x1, waiting for transfers between devices, per_device(): w_col = lax.all_gather(w_own, 'row', axis=0, tiled=True)  19.1 us
    dot_general x1, matrix products, per_device(): gradient = jnp.einsum('nsk,snl->skl', x_left, z_right, precision=HIGHEST)  15.8 us
    dot_general x1, matrix products, per_device(): jnp.einsum('snk,nsl->skl', z_left, x_right, precision=HIGHEST)  15 us
  transfers between devices with their start and end apart: 6, of which 6 were waited for; matrix products, arithmetic and copies ran while one was open for 17% of the time, Pallas kernels for 0%

commit v1 on v0

v1 whole, which is shorter than its diff:
```python
import functools

import jax
import jax.numpy as jnp
from jax import lax
from jax.experimental import pallas as pl
from jax.experimental.pallas import tpu as pltpu
from jax.sharding import PartitionSpec as P

MESH = pl.DeviceIdType.MESH
F32 = jnp.float32
BF16 = jnp.bfloat16
STEP_SIZE = 0.05
PENALTY = 4.0
SIDE = 4
NN = (((1,), (0,)), ((), ()))
NT = (((1,), (1,)), ((), ()))
TN = (((0,), (0,)), ((), ()))
ROUTES = ((True, 1), (True, -1), (False, 1), (False, -1))


def split(v):
    high = v.astype(BF16)
    low = (v - high.astype(F32)).astype(BF16)
    return high, low


def dot3(a, b, dims):
    ah, al = split(a)
    bh, bl = split(b)
    dot = functools.partial(lax.dot_general, dimension_numbers=dims, preferred_element_type=F32)
    return dot(ah, bh) + dot(ah, bl) + dot(al, bh)


def mod4(v):
    return lax.rem(v + 2 * SIDE, SIDE)


def shrink(v, limit):
    return jnp.where(v > 0, 1.0, -1.0) * jnp.maximum(jnp.abs(v) - limit, 0.0)


def kernel(
    xt, tiles_hbm, diag_ref, left, right, active, out_hbm, diag_out,
    xrow, xcol, zrow, zcol, tile, pw, py, rs0, rsb, rsa, ys, yx, yr, ids, lists,
    xa_s, xa_r, xb_s, xb_r, za_s, za_r, zb_s, zb_r, wa_s, wa_r, wb_s, wb_r,
    xh_s, xh_r, xp_s, xp_r, zh_s, zh_r, zp_s, zp_r, yh_s, yh_r, yp_s, yp_r,
    in_sem, out_sem,
):
    slots = left.shape[0]
    side, samp = xt.shape
    quarter, half = side // 4, side // 2
    r = lax.axis_index("row")
    c = lax.axis_index("col")
    x, core = lax.div(r, 2), lax.rem(r, 2)
    yy, zz = lax.div(c, SIDE), lax.rem(c, SIDE)
    other = 1 - core
    partner = 2 * x + other
    pos_a = [zz if first else yy for first, _ in ROUTES]
    pos_b = [yy if first else zz for first, _ in ROUTES]

    def col_of(q, a, b):
        return b * SIDE + a if ROUTES[q][0] else a * SIDE + b

    def qrows(q):
        return pl.ds(q * quarter, quarter)

    def hrows(g):
        return pl.ds(g * half, half)

    def remote(src, dst, send, recv, row, col):
        return pltpu.make_async_remote_copy(
            src_ref=src, dst_ref=dst, send_sem=send, recv_sem=recv,
            device_id=(row, col), device_id_type=MESH,
        )

    def next_a(q):
        return col_of(q, mod4(pos_a[q] + ROUTES[q][1]), pos_b[q])

    def next_b(q):
        return col_of(q, pos_a[q], mod4(pos_b[q] + ROUTES[q][1]))

    def next_x(g):
        return 2 * mod4(x + (1, -1)[g]) + core

    barrier = pltpu.get_barrier_semaphore()
    peers = [(r, next_a(q)) for q in range(4)]
    peers += [(next_x(0), c), (next_x(1), c), (partner, c)]
    for row, col in peers:
        pl.semaphore_signal(barrier, inc=1, device_id=(row, col), device_id_type=MESH)
    pl.semaphore_wait(barrier, len(peers))

    def gather_a(panel, q, h, own, sems):
        d = ROUTES[q][1]
        at = col_of(q, mod4(pos_a[q] - d * h), pos_b[q])
        src = own.at[qrows(q)] if h == 0 else panel.at[at, qrows(q)]
        return remote(src, panel.at[at, qrows(q)], sems[0].at[q, h], sems[1].at[q, h], r, next_a(q))

    def gather_a_arrival(panel, q, h, sems):
        d = ROUTES[q][1]
        at = col_of(q, mod4(pos_a[q] - d * (h + 1)), pos_b[q])
        ref = panel.at[at, qrows(q)]
        return remote(ref, ref, sems[0].at[q, h], sems[1].at[q, h], r, next_a(q))

    def gather_b(panel, q, i, own, sems):
        d = ROUTES[q][1]
        at = col_of(q, mod4(pos_a[q] - d * lax.rem(i, 4)), mod4(pos_b[q] - d * lax.div(i, 4)))
        src = panel.at[at, qrows(q)] if own is None else own.at[qrows(q)]
        return remote(src, panel.at[at, qrows(q)], sems[2].at[q, i], sems[3].at[q, i], r, next_b(q))

    def gather_b_arrival(panel, q, i, sems):
        d = ROUTES[q][1]
        at = col_of(q, mod4(pos_a[q] - d * lax.rem(i, 4)), mod4(pos_b[q] - d * (lax.div(i, 4) + 1)))
        ref = panel.at[at, qrows(q)]
        return remote(ref, ref, sems[2].at[q, i], sems[3].at[q, i], r, next_b(q))

    def ring(panel, g, h, own, sems):
        at = 2 * mod4(x - (1, -1)[g] * h) + core
        src = own.at[hrows(g)] if h == 0 else panel.at[at, hrows(g)]
        return remote(src, panel.at[at, hrows(g)], sems[0].at[g, h], sems[1].at[g, h], next_x(g), c)

    def ring_arrival(panel, g, h, sems):
        at = 2 * mod4(x - (1, -1)[g] * (h + 1)) + core
        ref = panel.at[at, hrows(g)]
        return remote(ref, ref, sems[0].at[g, h], sems[1].at[g, h], next_x(g), c)

    def hand(panel, g, h, own, sems):
        at = 2 * mod4(x - (1, -1)[g] * h) + core
        src = own.at[hrows(g)] if h == 0 else panel.at[at, hrows(g)]
        return remote(src, panel.at[at, hrows(g)], sems[2].at[g, h], sems[3].at[g, h], partner, c)

    def hand_arrival(panel, g, h, sems):
        at = 2 * mod4(x - (1, -1)[g] * h) + other
        ref = panel.at[at, hrows(g)]
        return remote(ref, ref, sems[2].at[g, h], sems[3].at[g, h], partner, c)

    def gather_phase(rowp, colp, own_row, own_col, csems, rsems, work, between, first_work):
        for q in range(4):
            gather_a(rowp, q, 0, own_row, csems).start()
        for g in range(2):
            ring(colp, g, 0, own_col, rsems).start()
            hand(colp, g, 0, own_col, rsems).start()
        for q in range(4):
            gather_b(rowp, q, 0, own_row, csems).start()
        first_work()

        def hop_a(h):
            for q in range(4):
                gather_a_arrival(rowp, q, h, csems).wait_recv()
                if h < 2:
                    gather_a(rowp, q, h + 1, own_row, csems).start()
                gather_b(rowp, q, h + 1, None, csems).start()

        def hop_x(h):
            for g in range(2):
                ring_arrival(colp, g, h, rsems).wait_recv()
                if h < 2:
                    ring(colp, g, h + 1, own_col, rsems).start()
                hand(colp, g, h + 1, own_col, rsems).start()

        def hop_b(i, forward):
            for q in range(4):
                gather_b_arrival(rowp, q, i, csems).wait_recv()
                if forward:
                    gather_b(rowp, q, i + 4, None, csems).start()

        hop_a(0)
        hop_a(1)
        hop_x(0)
        hop_a(2)
        hop_x(1)
        hop_b(0, True)
        hop_b(1, True)
        hop_x(2)
        hop_b(2, True)
        hop_b(3, True)
        for g in range(2):
            for h in range(4):
                hand_arrival(colp, g, h, rsems).wait_recv()

        @pl.loop(0, 4)
        def _(i):
            hop_b(i + 4, True)
            for k in range(4):
                work(i * 4 + k)

        between()

        @pl.loop(8, 12)
        def _(i):
            hop_b(i, False)

    def gather_drain(rowp, colp, own_row, own_col, csems, rsems):
        for q in range(4):
            for h in range(3):
                gather_a(rowp, q, h, own_row, csems).wait_send()

        @pl.loop(0, 12)
        def _(i):
            for q in range(4):
                gather_b(rowp, q, i, None, csems).wait_send()

        for g in range(2):
            for h in range(3):
                ring(colp, g, h, own_col, rsems).wait_send()
            for h in range(4):
                hand(colp, g, h, own_col, rsems).wait_send()

    def w_sum(col, rows):
        packed = lists[0, col]
        total = pw[packed & 15, rows, :]
        for j in range(1, 4):
            total = total + pw[lax.shift_right_arithmetic(packed, 4 * j) & 15, rows, :]
        return total

    def y_sum(row, rows):
        packed = lists[1, row]
        total = py[packed & 15, rows, :]
        for j in range(1, 8):
            total = total + py[lax.shift_right_arithmetic(packed, 4 * j) & 15, rows, :]
        return total

    def tile_in(s):
        return pltpu.make_async_copy(tiles_hbm.at[s], tile.at[s], in_sem.at[s])

    xsem = (xa_s, xa_r, xb_s, xb_r)
    zsem = (za_s, za_r, zb_s, zb_r)
    xrsem = (xh_s, xh_r, xp_s, xp_r)
    zrsem = (zh_s, zh_r, zp_s, zp_r)

    def start_work():
        for s in range(slots):
            tile_in(s).start()
        xrow[c] = xt[...]
        xcol[r] = xt[...]
        tile[slots] = diag_ref[...]
        pw[0] = jnp.zeros((side, samp), F32)
        py[0] = jnp.zeros((side, samp), F32)
        for s in range(slots):
            ids[0, s] = left[s]
            ids[1, s] = right[s]
            ids[2, s] = active[s]
        ids[0, slots] = c
        ids[1, slots] = r
        ids[2, slots] = 1

        def packs(which, n):
            @pl.loop(0, n)
            def _(a):
                packed = jnp.int32(0)
                for s in range(slots):
                    ident = left[s] if which == 0 else right[s]
                    packed = jnp.where(ident == a, packed * 16 + (s + 1), packed)
                lists[which, a] = packed

        packs(0, 16)
        packs(1, 8)
        for s in range(slots):
            tile_in(s).wait()

    def w_product(s):
        pw[s + 1] = dot3(tile[s], xcol[ids[1, s]], NN)

    def y_product(s):
        py[s + 1] = dot3(tile[s], xrow[ids[0, s]], TN)

    def scatter_target(q, h, j):
        d = ROUTES[q][1]
        return col_of(q, mod4(pos_a[q] - d * (j + 1)), mod4(pos_b[q] - d * (h + 1)))

    def scatter_b0(q, j):
        return remote(rs0.at[q, j], rsb.at[q, j], wb_s.at[q, j], wb_r.at[q, j], r, next_b(q))

    def scatter_b(q, i):
        return remote(rsb.at[q, i], rsb.at[q, i + 4], wb_s.at[q, i + 4], wb_r.at[q, i + 4], r, next_b(q))

    def scatter_b_arrival(q, i):
        return remote(rsb.at[q, i], rsb.at[q, i], wb_s.at[q, i], wb_r.at[q, i], r, next_b(q))

    def scatter_a(q, h):
        src = rsb.at[q, 8] if h == 0 else rsa.at[q, h - 1]
        return remote(src, rsa.at[q, h], wa_s.at[q, h], wa_r.at[q, h], r, next_a(q))

    def scatter_a_arrival(q, h):
        return remote(rsa.at[q, h], rsa.at[q, h], wa_s.at[q, h], wa_r.at[q, h], r, next_a(q))

    def scatter_start():
        for j in range(4):
            for q in range(4):
                rs0[q, j] = w_sum(scatter_target(q, 0, j), qrows(q))
            for q in range(4):
                scatter_b0(q, j).start()

    def scatter_hop(i, forward):
        h, j = lax.div(i, 4) + 1, lax.rem(i, 4)
        for q in range(4):
            scatter_b_arrival(q, i).wait_recv()
            rsb[q, i] = rsb[q, i] + w_sum(scatter_target(q, h, j), qrows(q))
            if forward:
                scatter_b(q, i).start()

    def y_target(g, h):
        return mod4(x - (1, -1)[g] * (h + 1))

    def y_give(g, h):
        return remote(ys.at[g, h], yx.at[g, h], yp_s.at[g, h], yp_r.at[g, h], partner, c)

    def y_ring(g, h):
        src = yx.at[g, 0] if h == 0 else yr.at[g, h - 1]
        return remote(src, yr.at[g, h], yh_s.at[g, h], yh_r.at[g, h], next_x(g), c)

    def y_exchange(h):
        for g in range(2):
            ys[g, h] = y_sum(2 * y_target(g, h) + other, hrows(g))
        for g in range(2):
            y_give(g, h).start()

    def y_combine(h):
        for g in range(2):
            y_give(g, h).wait_recv()
            yx[g, h] = yx[g, h] + y_sum(2 * y_target(g, h) + core, hrows(g))
        if h == 0:
            for g in range(2):
                y_ring(g, 0).start()

    def y_hop(h):
        for g in range(2):
            y_ring(g, h - 1).wait_recv()
            yr[g, h - 1] = yr[g, h - 1] + yx[g, h]
            if h < 3:
                y_ring(g, h).start()

    gather_phase(xrow, xcol, xt, xt, xsem, xrsem, w_product, scatter_start, start_work)

    @pl.loop(0, 4)
    def _(i):
        scatter_hop(i, True)
        for k in range(4):
            y_product(jnp.minimum(i * 4 + k, slots - 1))

    for h in range(4):
        y_exchange(h)
    scatter_hop(4, True)
    y_combine(0)
    scatter_hop(5, True)
    y_combine(1)
    scatter_hop(6, True)
    y_combine(2)
    y_combine(3)
    scatter_hop(7, True)
    y_hop(1)
    scatter_hop(8, False)
    for q in range(4):
        scatter_a(q, 0).start()
    scatter_hop(9, False)
    y_hop(2)
    for h in range(1, 3):
        if h == 2:
            scatter_hop(10, False)
        for q in range(4):
            scatter_a_arrival(q, h - 1).wait_recv()
            rsa[q, h - 1] = rsa[q, h - 1] + rsb[q, 8 + h]
            scatter_a(q, h).start()
    scatter_hop(11, False)
    y_hop(3)
    for q in range(4):
        scatter_a_arrival(q, 2).wait_recv()
        part = pl.ds((q % 2) * quarter, quarter)
        total = rsa[q, 2] + rsb[q, 11] + yr[q // 2, 2, part, :] + pw[slots + 1, qrows(q), :]
        zrow[c, qrows(q), :] = total
        zcol[r, qrows(q), :] = total

    scale = STEP_SIZE / (2.0 * samp)

    def first_half(s):
        factor = scale * ids[2, s].astype(F32)
        grad = dot3(xrow[ids[0, s]], zcol[ids[1, s]], NT)
        tile[s] = tile[s] - factor * grad

    gather_phase(
        zrow, zcol, zrow.at[c], zcol.at[r], zsem, zrsem, first_half, lambda: None, lambda: None
    )

    def tile_out(s):
        return pltpu.make_async_copy(tile.at[s], out_hbm.at[s], out_sem.at[s])

    def second_half(s):
        factor = scale * ids[2, s].astype(F32)
        grad = dot3(zrow[ids[0, s]], xcol[ids[1, s]], NT)
        return tile[s] - factor * grad

    @pl.loop(0, slots)
    def _(s):
        limit = STEP_SIZE * PENALTY * ids[2, s].astype(F32)
        tile[s] = shrink(second_half(s), limit)
        tile_out(s).start()

    stepped = second_half(slots)
    eye = lax.broadcasted_iota(jnp.int32, (side, side), 0) == lax.broadcasted_iota(
        jnp.int32, (side, side), 1
    )
    inverse = STEP_SIZE / jnp.where(eye, diag_ref[...], 1.0)
    diag_out[...] = jnp.where(eye, stepped + inverse, shrink(stepped, STEP_SIZE * PENALTY))

    gather_drain(xrow, xcol, xt, xt, xsem, xrsem)
    gather_drain(zrow, zcol, zrow.at[c], zcol.at[r], zsem, zrsem)
    for q in range(4):
        for j in range(4):
            scatter_b0(q, j).wait_send()
        for i in range(8):
            scatter_b(q, i).wait_send()
        for h in range(3):
            scatter_a(q, h).wait_send()
    for g in range(2):
        for h in range(4):
            y_give(g, h).wait_send()
        for h in range(3):
            y_ring(g, h).wait_send()
    for s in range(slots):
        tile_out(s).wait()


def per_device(samples, omega_tiles, omega_diag, tile_rows, tile_cols, tile_active):
    rows, cols = lax.axis_size("row"), lax.axis_size("col")
    samp, side = samples.shape
    slots = omega_tiles.shape[2]
    block = (side, samp)
    dma = pltpu.SemaphoreType.DMA
    vmem = pl.BlockSpec(memory_space=pltpu.VMEM)
    smem = pl.BlockSpec(memory_space=pltpu.SMEM)
    anyw = pl.BlockSpec(memory_space=pl.ANY)
    gather = [dma((4, 3)), dma((4, 3)), dma((4, 12)), dma((4, 12))]
    line = [dma((2, 3)), dma((2, 3)), dma((2, 4)), dma((2, 4))]
    new_tiles, new_diag = pl.pallas_call(
        kernel,
        out_shape=(
            jax.ShapeDtypeStruct((slots, side, side), F32),
            jax.ShapeDtypeStruct((side, side), F32),
        ),
        in_specs=[vmem, anyw, vmem, smem, smem, smem],
        out_specs=(anyw, vmem),
        scratch_shapes=[
            pltpu.VMEM((cols,) + block, F32),
            pltpu.VMEM((rows,) + block, F32),
            pltpu.VMEM((cols,) + block, F32),
            pltpu.VMEM((rows,) + block, F32),
            pltpu.VMEM((slots + 1, side, side), F32),
            pltpu.VMEM((slots + 2,) + block, F32),
            pltpu.VMEM((slots + 1,) + block, F32),
            pltpu.VMEM((4, 4, side // 4, samp), F32),
            pltpu.VMEM((4, 12, side // 4, samp), F32),
            pltpu.VMEM((4, 3, side // 4, samp), F32),
            pltpu.VMEM((2, 4, side // 2, samp), F32),
            pltpu.VMEM((2, 4, side // 2, samp), F32),
            pltpu.VMEM((2, 3, side // 2, samp), F32),
            pltpu.SMEM((3, slots + 1), jnp.int32),
            pltpu.SMEM((2, 16), jnp.int32),
        ]
        + gather + gather + gather + line + line + line
        + [dma((slots,)), dma((slots,))],
        compiler_params=pltpu.CompilerParams(
            collective_id=0, has_side_effects=True, vmem_limit_bytes=62 * 1024 * 1024
        ),
    )(
        samples.T,
        omega_tiles.reshape(slots, side, side),
        omega_diag,
        tile_rows.reshape(slots),
        tile_cols.reshape(slots),
        tile_active.reshape(slots),
    )
    return new_tiles[None, None], new_diag


def solution(mesh):
    in_specs = (
        P(None, ("row", "col")),
        P("row", "col", None, None, None),
        P(("row", "col"), None),
        P("row", "col", None),
        P("row", "col", None),
        P("row", "col", None),
    )
    out_specs = (P("row", "col", None, None, None), P(("row", "col"), None))
    return jax.shard_map(
        per_device, mesh=mesh, in_specs=in_specs, out_specs=out_specs, check_vma=False
    )
```

time: 464 us -> 137 us (0.30); the launches traced: 458 us -> 136 us
  waiting for transfers between devices: 307 us -> 0 us
  Pallas kernels: 0 us -> 129 us
  matrix products: 69.7 us -> 0 us
  local copies, waits for them, and re-layouts: 46.5 us -> 7.05 us
  other arithmetic: 20 us -> 0 us
  between operations: 14.5 us -> 0.65 us
    psum x2 -> x0, waiting for transfers between devices: 165 us -> none  [the longest x1 94.9 us: per_device(): w_full = lax.psum(w_part, 'col')]
    all_gather x4 -> x0, waiting for transfers between devices: 141 us -> none  [the longest x1 54.7 us: per_device(): y_row = lax.all_gather(y_own, 'col', axis=0, tiled=True)]
    pallas_call x0 -> x1, Pallas kernels: none -> 129 us  [per_device(): pl.pallas_call(kernel, out_shape=(jax.ShapeDtypeStruct((slots, side, side...]
    dot_general x8 -> x0, matrix products: 69.7 us -> none  [the longest x1 15.8 us: per_device(): gradient = jnp.einsum('nsk,snl->skl', x_left, z_right, precision=HIGHEST)]
    gather x5 -> x0, local copies, waits for them, and re-layouts: 22.7 us -> none  [the longest x1 6.84 us: per_device(): x_left = jnp.take(row_panel, left_ids, axis=1)]
    add x3 -> x0, other arithmetic: 16.8 us -> none  [the longest x1 8.45 us: per_device(): z_row = w_full + y_row]
    reshape x2 -> x0, local copies, waits for them, and re-layouts: 8.97 us -> none  [the longest x1 6.6 us: per_device(): lax.all_gather(samples, 'col', axis=1, tiled=True)]
    add x2 -> x0, local copies, waits for them, and re-layouts: 7.72 us -> none  [the longest x1 6.71 us: per_device(): z_row = w_full + y_row]
  transfers between devices with their start and end apart: 6 -> 0, of which waited for: 6 -> 0; matrix products, arithmetic and copies ran while one was open for 17% -> 0% of each run, Pallas kernels for 0% -> 0%
where the time goes in v1:
time: 137 us; the launch traced here: 136 us
  Pallas kernels  129 us (94%)
  local copies, waits for them, and re-layouts  7.05 us (5%)
    pallas_call x1, Pallas kernels, per_device(): pl.pallas_call(kernel, out_shape=(jax.ShapeDtypeStruct((slots, side, side...  129 us
    unnamed x5, local copies, waits for them, and re-layouts  7.05 us

profile of v1, /device:TPU:1, one launch (start us, length us, event | category | flops | bytes accessed | tf_op | source)
XLA Modules:
  0.0 136.5 jit_solution(3615235069332582220)
XLA Ops:
  0.6 1.9 %copy.8 = f32[384,256]{0,1:T(8,128)} copy(f32[384,256]{1,0:T(8,128)} %param.6) | data formatting | bytes 786432 | tf_op args[0]
  2.5 128.8 %shard_map.77 = (f32[15,256,256]{2,1,0:T(8,128)}, f32[256,256]{1,0:T(8,128)}) custom-call(f32[256,384]{1,0:T(8,128)} %bitcast.8, f32[15,256,256]{2,1,0:T(8,128)} %bitcast.6, f32[256,256]{1,0:T(8,128)} %diag_ref.1, s32[15]{0:T(128)} %bitcast.9, s32[15]{0:T(128)} %bitcast.10, s32[15]{0:T(128)} %bitcast.11), custom_call_target="tpu_custom_call" | custom-call | tf_op jit(solution)/shard_map/pallas_call | solution.py:434
  131.3 0.0 copy-start
  131.4 4.4 %copy.11 = f32[1,1,15,256,256]{4,3,2,1,0:T(8,128)} copy(f32[1,1,15,256,256]{4,3,2,1,0:T(8,128)} %bitcast.7) | data formatting | bytes 7864320
  135.8 0.0 copy-done
  135.8 0.7 copy.12
Async XLA Ops:
  131.3 4.4 %copy-start = (f32[256,256]{1,0:T(8,128)S(1)}, f32[256,256]{1,0:T(8,128)}, u32[]{:S(2)}) copy-start(f32[256,256]{1,0:T(8,128)} %get-tuple-element.9) | copy-start | bytes 786436

commit v2 on v1

v2 whole, which is shorter than its diff:
```python
import functools

import jax
import jax.numpy as jnp
from jax import lax
from jax.experimental import pallas as pl
from jax.experimental.pallas import tpu as pltpu
from jax.sharding import PartitionSpec as P

MESH = pl.DeviceIdType.MESH
F32 = jnp.float32
BF16 = jnp.bfloat16
STEP_SIZE = 0.05
PENALTY = 4.0
SIDE = 4
NN = (((1,), (0,)), ((), ()))
NT = (((1,), (1,)), ((), ()))
TN = (((0,), (0,)), ((), ()))
ROUTES = ((True, 1), (True, -1), (False, 1), (False, -1))


def split(v):
    high = v.astype(BF16)
    low = (v - high.astype(F32)).astype(BF16)
    return high, low


def dot3(a, b, dims):
    ah, al = split(a)
    bh, bl = split(b)
    dot = functools.partial(lax.dot_general, dimension_numbers=dims, preferred_element_type=F32)
    return dot(ah, bh) + dot(ah, bl) + dot(al, bh)


def mod4(v):
    return lax.rem(v + 2 * SIDE, SIDE)


def shrink(v, limit):
    return jnp.where(v > 0, 1.0, -1.0) * jnp.maximum(jnp.abs(v) - limit, 0.0)


def kernel(
    samples_hbm, tiles_hbm, diag_hbm, left, right, active,
    tile, zh, zl, xh, xl, ids,
    raw, xt, xrow, xcol, zrow, zcol, pw, py, rs0, rsb, rsa, ys, yx, yr, lists,
    ga_r, gb_r, xf_r, zf_r, gh_r, gp_r, wa_r, wb_r, yh_r, yp_r,
    x_s, xr_s, z_s, zr_s, w_s, y_s, in_sem,
):
    slots = left.shape[0]
    samp, side = raw.shape
    quarter, half = side // 4, side // 2
    r = lax.axis_index("row")
    c = lax.axis_index("col")
    x, core = lax.div(r, 2), lax.rem(r, 2)
    yy, zz = lax.div(c, SIDE), lax.rem(c, SIDE)
    other = 1 - core
    partner = 2 * x + other
    pos_a = [zz if first else yy for first, _ in ROUTES]
    pos_b = [yy if first else zz for first, _ in ROUTES]

    def col_of(q, a, b):
        return b * SIDE + a if ROUTES[q][0] else a * SIDE + b

    def qrows(q):
        return pl.ds(q * quarter, quarter)

    def hrows(g):
        return pl.ds(g * half, half)

    def remote(src, dst, send, recv, row, col):
        return pltpu.make_async_remote_copy(
            src_ref=src, dst_ref=dst, send_sem=send, recv_sem=recv,
            device_id=(row, col), device_id_type=MESH,
        )

    def next_a(q):
        return col_of(q, mod4(pos_a[q] + ROUTES[q][1]), pos_b[q])

    def next_b(q):
        return col_of(q, pos_a[q], mod4(pos_b[q] + ROUTES[q][1]))

    def next_x(g):
        return 2 * mod4(x + (1, -1)[g]) + core

    barrier = pltpu.get_barrier_semaphore()
    peers = [(r, next_a(q)) for q in range(4)]
    peers += [(next_x(0), c), (next_x(1), c), (partner, c)]
    for row, col in peers:
        pl.semaphore_signal(barrier, inc=1, device_id=(row, col), device_id_type=MESH)
    loads = [
        pltpu.make_async_copy(samples_hbm, raw, in_sem.at[0]),
        pltpu.make_async_copy(tiles_hbm, tile.at[pl.ds(0, slots)], in_sem.at[1]),
        pltpu.make_async_copy(diag_hbm, tile.at[slots], in_sem.at[2]),
    ]
    for load in loads:
        load.start()
    loads[0].wait()
    own = raw[...].T
    xt[...] = own
    xrow[c] = own
    xcol[r] = own
    pw[0] = jnp.zeros((side, samp), F32)
    py[0] = jnp.zeros((side, samp), F32)
    pl.semaphore_wait(barrier, len(peers))

    def gather_a(panel, q, h, own, sems):
        d = ROUTES[q][1]
        at = col_of(q, mod4(pos_a[q] - d * h), pos_b[q])
        src = own.at[qrows(q)] if h == 0 else panel.at[at, qrows(q)]
        return remote(src, panel.at[at, qrows(q)], sems[0], ga_r.at[q, h], r, next_a(q))

    def gather_a_arrival(panel, q, h, sems):
        d = ROUTES[q][1]
        at = col_of(q, mod4(pos_a[q] - d * (h + 1)), pos_b[q])
        ref = panel.at[at, qrows(q)]
        return remote(ref, ref, sems[0], ga_r.at[q, h], r, next_a(q))

    def gather_b(panel, q, i, own, sems, last=False):
        d = ROUTES[q][1]
        at = col_of(q, mod4(pos_a[q] - d * lax.rem(i, 4)), mod4(pos_b[q] - d * lax.div(i, 4)))
        src = panel.at[at, qrows(q)] if own is None else own.at[qrows(q)]
        recv = sems[1] if last else gb_r.at[q, i]
        return remote(src, panel.at[at, qrows(q)], sems[0], recv, r, next_b(q))

    def arrived_b(q, i):
        d = ROUTES[q][1]
        return col_of(q, mod4(pos_a[q] - d * lax.rem(i, 4)), mod4(pos_b[q] - d * (lax.div(i, 4) + 1)))

    def gather_b_arrival(panel, q, i, sems):
        ref = panel.at[arrived_b(q, i), qrows(q)]
        return remote(ref, ref, sems[0], gb_r.at[q, i], r, next_b(q))

    def gather_last(panel, sems):
        ref = panel.at[pl.ds(0, 4)]
        return remote(ref, ref, sems[0], sems[1], r, next_b(0))

    def ring(panel, g, h, own, sems):
        at = 2 * mod4(x - (1, -1)[g] * h) + core
        src = own.at[hrows(g)] if h == 0 else panel.at[at, hrows(g)]
        return remote(src, panel.at[at, hrows(g)], sems[0], gh_r.at[g, h], next_x(g), c)

    def ring_arrival(panel, g, h, sems):
        at = 2 * mod4(x - (1, -1)[g] * (h + 1)) + core
        ref = panel.at[at, hrows(g)]
        return remote(ref, ref, sems[0], gh_r.at[g, h], next_x(g), c)

    def hand(panel, g, h, own, sems):
        at = 2 * mod4(x - (1, -1)[g] * h) + core
        src = own.at[hrows(g)] if h == 0 else panel.at[at, hrows(g)]
        return remote(src, panel.at[at, hrows(g)], sems[0], sems[1], partner, c)

    def hand_arrivals(panel, sems):
        ref = panel.at[pl.ds(0, 4)]
        return remote(ref, ref, sems[0], sems[1], partner, c)

    def gather_phase(rowp, colp, own_row, own_col, csems, rsems, first_work, seen, work, between):
        for q in range(4):
            gather_a(rowp, q, 0, own_row, csems).start()
        for g in range(2):
            ring(colp, g, 0, own_col, rsems).start()
            hand(colp, g, 0, own_col, rsems).start()
        for q in range(4):
            gather_b(rowp, q, 0, own_row, csems).start()
        first_work()

        def hop_a(h):
            for q in range(4):
                gather_a_arrival(rowp, q, h, csems).wait_recv()
                if h < 2:
                    gather_a(rowp, q, h + 1, own_row, csems).start()
            for q in range(4):
                gather_b(rowp, q, h + 1, None, csems).start()
            for q in range(4):
                seen(q, col_of(q, mod4(pos_a[q] - ROUTES[q][1] * (h + 1)), pos_b[q]))

        def hop_x(h):
            for g in range(2):
                ring_arrival(colp, g, h, rsems).wait_recv()
                if h < 2:
                    ring(colp, g, h + 1, own_col, rsems).start()
                hand(colp, g, h + 1, own_col, rsems).start()

        def hop_b(i, last):
            for q in range(4):
                gather_b_arrival(rowp, q, i, csems).wait_recv()
                gather_b(rowp, q, i + 4, None, csems, last).start()
            for q in range(4):
                seen(q, arrived_b(q, i))

        hop_a(0)
        hop_b(0, False)
        hop_x(0)
        hop_a(1)
        hop_b(1, False)
        hop_a(2)
        hop_x(1)
        hop_b(2, False)
        hop_b(3, False)
        hop_x(2)
        hop_b(4, True)
        hand_arrivals(colp, rsems).wait_recv()

        @pl.loop(0, 4)
        def _(i):
            for k in range(4):
                work(i * 4 + k)

            @pl.when(i < 3)
            def _():
                hop_b(i + 5, True)

        between()
        gather_last(rowp, csems).wait_recv()

        @pl.loop(8, 12)
        def _(i):
            for q in range(4):
                seen(q, arrived_b(q, i))

    def drain(ref, blocks, sem):
        ref = ref.at[pl.ds(0, blocks)]
        remote(ref, ref, sem, in_sem.at[0], partner, c).wait_send()

    def w_sum(col, rows):
        packed = lists[0, col]
        total = pw[packed & 15, rows, :]
        for j in range(1, 4):
            total = total + pw[lax.shift_right_arithmetic(packed, 4 * j) & 15, rows, :]
        return total

    def y_sum(row, rows):
        packed = lists[1, row]
        total = py[packed & 15, rows, :]
        for j in range(1, 8):
            total = total + py[lax.shift_right_arithmetic(packed, 4 * j) & 15, rows, :]
        return total

    xsem, zsem = (x_s, xf_r), (z_s, zf_r)
    xrsem, zrsem = (xr_s, gp_r.at[0]), (zr_s, gp_r.at[1])

    def start_work():
        for s in range(slots):
            ids[0, s] = left[s]
            ids[1, s] = right[s]
            ids[2, s] = active[s]
        ids[0, slots] = c
        ids[1, slots] = r
        ids[2, slots] = 1

        def packs(which, n):
            @pl.loop(0, n)
            def _(a):
                packed = jnp.int32(0)
                for s in range(slots):
                    ident = left[s] if which == 0 else right[s]
                    packed = jnp.where(ident == a, packed * 16 + (s + 1), packed)
                lists[which, a] = packed

        packs(0, 16)
        packs(1, 8)
        for load in loads[1:]:
            load.wait()

    def w_product(s):
        pw[s + 1] = dot3(tile[s], xcol[ids[1, s]], NN)

    def y_product(s):
        py[s + 1] = dot3(tile[s], xrow[ids[0, s]], TN)

    def scatter_target(q, h, j):
        d = ROUTES[q][1]
        return col_of(q, mod4(pos_a[q] - d * (j + 1)), mod4(pos_b[q] - d * (h + 1)))

    def scatter_b0(q, j):
        return remote(rs0.at[q, j], rsb.at[q, j], w_s, wb_r.at[q, j], r, next_b(q))

    def scatter_b(q, i):
        return remote(rsb.at[q, i], rsb.at[q, i + 4], w_s, wb_r.at[q, i + 4], r, next_b(q))

    def scatter_b_arrival(q, i):
        return remote(rsb.at[q, i], rsb.at[q, i], w_s, wb_r.at[q, i], r, next_b(q))

    def scatter_a(q, h):
        src = rsb.at[q, 8] if h == 0 else rsa.at[q, h - 1]
        return remote(src, rsa.at[q, h], w_s, wa_r.at[q, h], r, next_a(q))

    def scatter_a_arrival(q, h):
        return remote(rsa.at[q, h], rsa.at[q, h], w_s, wa_r.at[q, h], r, next_a(q))

    def scatter_start():
        for j in range(4):
            for q in range(4):
                rs0[q, j] = w_sum(scatter_target(q, 0, j), qrows(q))
            for q in range(4):
                scatter_b0(q, j).start()

    def scatter_hop(h, j):
        i = (h - 1) * 4 + j
        for q in range(4):
            scatter_b_arrival(q, i).wait_recv()
            rsb[q, i] = rsb[q, i] + w_sum(scatter_target(q, h, j), qrows(q))
        if h < 3:
            for q in range(4):
                scatter_b(q, i).start()

    def scatter_step(h):
        for q in range(4):
            scatter_a_arrival(q, h - 1).wait_recv()
            rsa[q, h - 1] = rsa[q, h - 1] + rsb[q, 8 + h]
        for q in range(4):
            scatter_a(q, h).start()

    def y_target(g, h):
        return mod4(x - (1, -1)[g] * (h + 1))

    def y_give(g, h):
        return remote(ys.at[g, h], yx.at[g, h], y_s, yp_r.at[g, h], partner, c)

    def y_ring(g, h):
        src = yx.at[g, 0] if h == 0 else yr.at[g, h - 1]
        return remote(src, yr.at[g, h], y_s, yh_r.at[g, h], next_x(g), c)

    def y_exchange(h):
        for g in range(2):
            ys[g, h] = y_sum(2 * y_target(g, h) + other, hrows(g))
        for g in range(2):
            y_give(g, h).start()

    def y_combine(h):
        for g in range(2):
            y_give(g, h).wait_recv()
            yx[g, h] = yx[g, h] + y_sum(2 * y_target(g, h) + core, hrows(g))
        if h == 0:
            for g in range(2):
                y_ring(g, 0).start()

    def y_hop(h):
        for g in range(2):
            y_ring(g, h - 1).wait_recv()
            yr[g, h - 1] = yr[g, h - 1] + yx[g, h]
            if h < 3:
                y_ring(g, h).start()

    gather_phase(
        xrow, xcol, xt, xt, xsem, xrsem, start_work, lambda q, at: None, w_product, scatter_start
    )

    def y_products(first):
        @pl.loop(0, 4)
        def _(k):
            y_product(jnp.minimum(first + k, slots - 1))

    for j in range(2):
        y_products(8 * j)
        scatter_hop(1, j)
        y_products(8 * j + 4)
    y_exchange(0)
    scatter_hop(2, 0)
    y_exchange(1)
    scatter_hop(1, 2)
    y_exchange(2)
    y_combine(0)
    scatter_hop(2, 1)
    y_exchange(3)
    scatter_hop(1, 3)
    y_combine(1)
    y_combine(2)
    y_combine(3)
    scatter_hop(3, 0)
    for q in range(4):
        scatter_a(q, 0).start()

    @pl.loop(0, 8)
    def _(b):
        xh[b], xl[b] = split(xcol[b])

    eye = lax.broadcasted_iota(jnp.int32, (side, side), 0) == lax.broadcasted_iota(
        jnp.int32, (side, side), 1
    )
    tile[slots] = tile[slots] + jnp.where(eye, STEP_SIZE / jnp.where(eye, tile[slots], 1.0), 0.0)
    scatter_hop(2, 2)
    y_hop(1)
    scatter_hop(3, 1)
    scatter_step(1)
    scatter_hop(2, 3)
    y_hop(2)
    scatter_hop(3, 2)
    scatter_step(2)
    scatter_hop(3, 3)
    y_hop(3)
    for q in range(4):
        scatter_a_arrival(q, 2).wait_recv()
        part = pl.ds((q % 2) * quarter, quarter)
        total = rsa[q, 2] + rsb[q, 11] + yr[q // 2, 2, part, :] + pw[slots + 1, qrows(q), :]
        zrow[c, qrows(q), :] = total
        zcol[r, qrows(q), :] = total

    scale = STEP_SIZE / (2.0 * samp)

    def first_half(s):
        factor = scale * ids[2, s].astype(F32)
        grad = dot3(xrow[ids[0, s]], zcol[ids[1, s]], NT)
        tile[s] = tile[s] - factor * grad

    def seen(q, at):
        zh[at, qrows(q), :], zl[at, qrows(q), :] = split(zrow[at, qrows(q), :])

    def own_seen():
        zh[c], zl[c] = split(zrow[c])

    gather_phase(
        zrow, zcol, zrow.at[c], zcol.at[r], zsem, zrsem, own_seen, seen, first_half, lambda: None
    )

    drain(xrow, 15, x_s)
    drain(xcol, 7, xr_s)
    drain(zrow, 15, z_s)
    drain(zcol, 7, zr_s)
    drain(xrow, 15, w_s)
    drain(xcol, 7, y_s)


def finish(tile, zh, zl, xh, xl, ids, out_hbm, diag_hbm, done, out_sem):
    slots = out_hbm.shape[0]
    side, samp = zh.shape[1:]
    scale = STEP_SIZE / (2.0 * samp)
    dot = functools.partial(lax.dot_general, dimension_numbers=NT, preferred_element_type=F32)

    def stepped(s):
        a, b = ids[0, s], ids[1, s]
        grad = dot(zh[a], xh[b]) + dot(zh[a], xl[b]) + dot(zl[a], xh[b])
        return tile[s] - scale * ids[2, s].astype(F32) * grad

    def out(s):
        return pltpu.make_async_copy(done.at[s], out_hbm.at[s], out_sem.at[s])

    def diag_out():
        return pltpu.make_async_copy(done.at[slots], diag_hbm, out_sem.at[slots])

    eye = lax.broadcasted_iota(jnp.int32, (side, side), 0) == lax.broadcasted_iota(
        jnp.int32, (side, side), 1
    )
    value = stepped(slots)
    done[slots] = jnp.where(eye, value, shrink(value, STEP_SIZE * PENALTY))
    diag_out().start()

    @pl.loop(0, slots)
    def _(s):
        done[s] = shrink(stepped(s), STEP_SIZE * PENALTY * ids[2, s].astype(F32))
        out(s).start()

    diag_out().wait()

    @pl.loop(0, slots)
    def _(s):
        out(s).wait()


def per_device(samples, omega_tiles, omega_diag, tile_rows, tile_cols, tile_active):
    rows, cols = lax.axis_size("row"), lax.axis_size("col")
    samp, side = samples.shape
    slots = omega_tiles.shape[2]
    block = (side, samp)
    dma = pltpu.SemaphoreType.DMA
    vmem = pl.BlockSpec(memory_space=pltpu.VMEM)
    smem = pl.BlockSpec(memory_space=pltpu.SMEM)
    anyw = pl.BlockSpec(memory_space=pl.ANY)
    middle = pl.pallas_call(
        kernel,
        out_shape=(
            pltpu.VMEM((slots + 1, side, side), F32),
            pltpu.VMEM((cols,) + block, BF16),
            pltpu.VMEM((cols,) + block, BF16),
            pltpu.VMEM((rows,) + block, BF16),
            pltpu.VMEM((rows,) + block, BF16),
            pltpu.SMEM((3, slots + 1), jnp.int32),
        ),
        in_specs=[anyw] * 3 + [smem] * 3,
        out_specs=(vmem,) * 5 + (smem,),
        scratch_shapes=[
            pltpu.VMEM((samp, side), F32),
            pltpu.VMEM(block, F32),
            pltpu.VMEM((cols,) + block, F32),
            pltpu.VMEM((rows,) + block, F32),
            pltpu.VMEM((cols,) + block, F32),
            pltpu.VMEM((rows,) + block, F32),
            pltpu.VMEM((slots + 2,) + block, F32),
            pltpu.VMEM((slots + 1,) + block, F32),
            pltpu.VMEM((4, 4, side // 4, samp), F32),
            pltpu.VMEM((4, 12, side // 4, samp), F32),
            pltpu.VMEM((4, 3, side // 4, samp), F32),
            pltpu.VMEM((2, 4, side // 2, samp), F32),
            pltpu.VMEM((2, 4, side // 2, samp), F32),
            pltpu.VMEM((2, 3, side // 2, samp), F32),
            pltpu.SMEM((2, 16), jnp.int32),
            dma((4, 3)), dma((4, 8)), dma(()), dma(()), dma((2, 3)), dma((2,)),
            dma((4, 3)), dma((4, 12)), dma((2, 3)), dma((2, 4)),
            dma(()), dma(()), dma(()), dma(()), dma(()), dma(()), dma((3,)),
        ],
        compiler_params=pltpu.CompilerParams(
            collective_id=0, has_side_effects=True, vmem_limit_bytes=48 * 1024 * 1024
        ),
    )(
        samples,
        omega_tiles.reshape(slots, side, side),
        omega_diag,
        tile_rows.reshape(slots),
        tile_cols.reshape(slots),
        tile_active.reshape(slots),
    )
    new_tiles, new_diag = pl.pallas_call(
        finish,
        out_shape=(
            jax.ShapeDtypeStruct((slots, side, side), F32),
            jax.ShapeDtypeStruct((side, side), F32),
        ),
        in_specs=[vmem] * 5 + [smem],
        out_specs=(anyw, anyw),
        scratch_shapes=[pltpu.VMEM((slots + 1, side, side), F32), dma((slots + 1,))],
        compiler_params=pltpu.CompilerParams(vmem_limit_bytes=16 * 1024 * 1024),
    )(*middle)
    return new_tiles[None, None], new_diag


def solution(mesh):
    in_specs = (
        P(None, ("row", "col")),
        P("row", "col", None, None, None),
        P(("row", "col"), None),
        P("row", "col", None),
        P("row", "col", None),
        P("row", "col", None),
    )
    out_specs = (P("row", "col", None, None, None), P(("row", "col"), None))
    return jax.shard_map(
        per_device, mesh=mesh, in_specs=in_specs, out_specs=out_specs, check_vma=False
    )
```

time: 137 us -> 120 us (0.88)
  Pallas kernels: 129 us -> 119 us
  local copies, waits for them, and re-layouts: 7.05 us -> 0 us
    pallas_call x1 -> x2, Pallas kernels: 129 us -> 119 us  [the longest x1 112 us: per_device(): pl.pallas_call(kernel, out_shape=(pltpu.VMEM((slots + 1, side, side), F32...]
    unnamed x5 -> x0, local copies, waits for them, and re-layouts: 7.05 us -> none
where the time goes in v2:
time: 120 us
  Pallas kernels  119 us (99%)
    pallas_call x1, Pallas kernels, per_device(): pl.pallas_call(kernel, out_shape=(pltpu.VMEM((slots + 1, side, side), F32...  112 us
    pallas_call x1, Pallas kernels, per_device(): pl.pallas_call(finish, out_shape=(jax.ShapeDtypeStruct((slots, side, side...  7.46 us

profile of v2, /device:TPU:1, one launch (start us, length us, event | category | flops | bytes accessed | tf_op | source)
XLA Modules:
  0.0 119.7 jit_solution(17698123698958705998)
XLA Ops:
  0.6 111.6 %shard_map.77 = (f32[16,256,256]{2,1,0:T(8,128)S(1)}, bf16[16,256,384]{2,1,0:T(8,128)(2,1)S(1)}, bf16[16,256,384]{2,1,0:T(8,128)(2,1)S(1)}, bf16[8,256,384]{2,1,...) custom-call(f32[384,256]{1,0:T(8,128)} %samples_hbm.1, f32[15,256,256]{2,1,0:T(8,128)} %bitcast.5, ...), custom_call_target="tpu_custom_call" | custom-call | tf_op jit(solution)/shard_map/pallas_call | solution.py:469
  112.3 7.5 %shard_map.78 = (f32[15,256,256]{2,1,0:T(8,128)}, f32[256,256]{1,0:T(8,128)}) custom-call(f32[16,256,256]{2,1,0:T(8,128)S(1)} %get-tuple-element.10.tile, bf16[16,256,384]{2,1,0:T(8,128)(2,1)S(1)} %get-tuple-element.11.zh, bf16[16,256,384]{2,1,0:T(8,128)(2,1)S(1)} %get-tuple-element.12.zl, bf16[8,256,384]{2,1,0:T(8,128)(2,1)S(1)} %get-tuple-element.13.xh, ...), custom_call_target="tpu_custom_call" | custom-call | tf_op jit(solution)/shard_map/pallas_call | solution.py:512

commit v3 on v2

--- a/solution.py
+++ b/solution.py
@@ -373,7 +373,7 @@
 
     @pl.loop(0, 8)
     def _(b):
-        xh[b], xl[b] = split(xcol[b])
+        xh[b], xl[b] = split(xcol[b].T)
 
     eye = lax.broadcasted_iota(jnp.int32, (side, side), 0) == lax.broadcasted_iota(
         jnp.int32, (side, side), 1
@@ -425,7 +425,7 @@
     slots = out_hbm.shape[0]
     side, samp = zh.shape[1:]
     scale = STEP_SIZE / (2.0 * samp)
-    dot = functools.partial(lax.dot_general, dimension_numbers=NT, preferred_element_type=F32)
+    dot = functools.partial(lax.dot_general, dimension_numbers=NN, preferred_element_type=F32)
 
     def stepped(s):
         a, b = ids[0, s], ids[1, s]
@@ -433,10 +433,10 @@
         return tile[s] - scale * ids[2, s].astype(F32) * grad
 
     def out(s):
-        return pltpu.make_async_copy(done.at[s], out_hbm.at[s], out_sem.at[s])
+        return pltpu.make_async_copy(done.at[s], out_hbm.at[s], out_sem)
 
     def diag_out():
-        return pltpu.make_async_copy(done.at[slots], diag_hbm, out_sem.at[slots])
+        return pltpu.make_async_copy(done.at[slots], diag_hbm, out_sem)
 
     eye = lax.broadcasted_iota(jnp.int32, (side, side), 0) == lax.broadcasted_iota(
         jnp.int32, (side, side), 1
@@ -445,16 +445,11 @@
     done[slots] = jnp.where(eye, value, shrink(value, STEP_SIZE * PENALTY))
     diag_out().start()
 
-    @pl.loop(0, slots)
-    def _(s):
+    for s in range(slots):
         done[s] = shrink(stepped(s), STEP_SIZE * PENALTY * ids[2, s].astype(F32))
         out(s).start()
 
-    diag_out().wait()
-
-    @pl.loop(0, slots)
-    def _(s):
-        out(s).wait()
+    pltpu.make_async_copy(done, done, out_sem).wait()
 
 
 def per_device(samples, omega_tiles, omega_diag, tile_rows, tile_cols, tile_active):
@@ -472,8 +467,8 @@
             pltpu.VMEM((slots + 1, side, side), F32),
             pltpu.VMEM((cols,) + block, BF16),
             pltpu.VMEM((cols,) + block, BF16),
-            pltpu.VMEM((rows,) + block, BF16),
-            pltpu.VMEM((rows,) + block, BF16),
+            pltpu.VMEM((rows, samp, side), BF16),
+            pltpu.VMEM((rows, samp, side), BF16),
             pltpu.SMEM((3, slots + 1), jnp.int32),
         ),
         in_specs=[anyw] * 3 + [smem] * 3,
@@ -517,7 +512,7 @@
         ),
         in_specs=[vmem] * 5 + [smem],
         out_specs=(anyw, anyw),
-        scratch_shapes=[pltpu.VMEM((slots + 1, side, side), F32), dma((slots + 1,))],
+        scratch_shapes=[pltpu.VMEM((slots + 1, side, side), F32), dma(())],
         compiler_params=pltpu.CompilerParams(vmem_limit_bytes=16 * 1024 * 1024),
     )(*middle)
     return new_tiles[None, None], new_diag

time: 120 us -> 117 us (0.975)
  Pallas kernels: 119 us -> 116 us
    pallas_call x1, Pallas kernels: 7.46 us -> 4.36 us  [per_device(): pl.pallas_call(finish, out_shape=(jax.ShapeDtypeStruct((slots, side, side...]
where the time goes in v3:
time: 117 us
  Pallas kernels  116 us (99%)
    pallas_call x1, Pallas kernels, per_device(): pl.pallas_call(kernel, out_shape=(pltpu.VMEM((slots + 1, side, side), F32...  112 us
    pallas_call x1, Pallas kernels, per_device(): pl.pallas_call(finish, out_shape=(jax.ShapeDtypeStruct((slots, side, side...  4.36 us

profile of v3, /device:TPU:1, one launch (start us, length us, event | category | flops | bytes accessed | tf_op | source)
XLA Modules:
  0.0 116.6 jit_solution(13281418293034089514)
XLA Ops:
  0.6 111.6 %shard_map.77 = (f32[16,256,256]{2,1,0:T(8,128)S(1)}, bf16[16,256,384]{2,1,0:T(8,128)(2,1)S(1)}, bf16[16,256,384]{2,1,0:T(8,128)(2,1)S(1)}, bf16[8,384,256]{2,1,...) custom-call(f32[384,256]{1,0:T(8,128)} %samples_hbm.1, f32[15,256,256]{2,1,0:T(8,128)} %bitcast.5, ...), custom_call_target="tpu_custom_call" | custom-call | tf_op jit(solution)/shard_map/pallas_call | solution.py:464
  112.3 4.4 %shard_map.78 = (f32[15,256,256]{2,1,0:T(8,128)}, f32[256,256]{1,0:T(8,128)}) custom-call(f32[16,256,256]{2,1,0:T(8,128)S(1)} %get-tuple-element.10.tile, bf16[16,256,384]{2,1,0:T(8,128)(2,1)S(1)} %get-tuple-element.11.zh, bf16[16,256,384]{2,1,0:T(8,128)(2,1)S(1)} %get-tuple-element.12.zl, bf16[8,384,256]{2,1,0:T(8,128)(2,1)S(1)} %get-tuple-element.13.xh, ...), custom_call_target="tpu_custom_call" | custom-call | tf_op jit(solution)/shard_map/pallas_call | solution.py:507

commit v4 on v3

--- a/solution.py
+++ b/solution.py
@@ -41,13 +41,13 @@
 
 
 def kernel(
-    samples_hbm, tiles_hbm, diag_hbm, left, right, active,
+    samples_hbm, tiles_hbm, diag_hbm, left_hbm, right_hbm, active_hbm,
     tile, zh, zl, xh, xl, ids,
-    raw, xt, xrow, xcol, zrow, zcol, pw, py, rs0, rsb, rsa, ys, yx, yr, lists,
+    raw, xt, xrow, xcol, zrow, zcol, pw, py, rs0, rsb, rsa, ys, yx, yr, lists, idv0, idv1, idv2, idv, named,
     ga_r, gb_r, xf_r, zf_r, gh_r, gp_r, wa_r, wb_r, yh_r, yp_r,
     x_s, xr_s, z_s, zr_s, w_s, y_s, in_sem,
 ):
-    slots = left.shape[0]
+    slots = left_hbm.shape[0]
     samp, side = raw.shape
     quarter, half = side // 4, side // 2
     r = lax.axis_index("row")
@@ -92,6 +92,9 @@
         pltpu.make_async_copy(samples_hbm, raw, in_sem.at[0]),
         pltpu.make_async_copy(tiles_hbm, tile.at[pl.ds(0, slots)], in_sem.at[1]),
         pltpu.make_async_copy(diag_hbm, tile.at[slots], in_sem.at[2]),
+        pltpu.make_async_copy(left_hbm, idv0, in_sem.at[3]),
+        pltpu.make_async_copy(right_hbm, idv1, in_sem.at[4]),
+        pltpu.make_async_copy(active_hbm, idv2, in_sem.at[5]),
     ]
     for load in loads:
         load.start()
@@ -154,7 +157,7 @@
         ref = panel.at[pl.ds(0, 4)]
         return remote(ref, ref, sems[0], sems[1], partner, c)
 
-    def gather_phase(rowp, colp, own_row, own_col, csems, rsems, first_work, seen, work, between):
+    def gather_phase(rowp, colp, own_row, own_col, csems, rsems, first_work, seen, work, early, between):
         for q in range(4):
             gather_a(rowp, q, 0, own_row, csems).start()
         for g in range(2):
@@ -188,28 +191,29 @@
             for q in range(4):
                 seen(q, arrived_b(q, i))
 
+        def works(first, last):
+            @pl.loop(first // 4, last // 4)
+            def _(i):
+                for k in range(4):
+                    work(i * 4 + k)
+
         hop_a(0)
         hop_b(0, False)
+        hop_a(1)
         hop_x(0)
-        hop_a(1)
         hop_b(1, False)
         hop_a(2)
+        hop_b(2, False)
         hop_x(1)
-        hop_b(2, False)
         hop_b(3, False)
+        hop_b(4, True)
+        hop_b(5, True)
         hop_x(2)
-        hop_b(4, True)
+        hop_b(6, True)
         hand_arrivals(colp, rsems).wait_recv()
-
-        @pl.loop(0, 4)
-        def _(i):
-            for k in range(4):
-                work(i * 4 + k)
-
-            @pl.when(i < 3)
-            def _():
-                hop_b(i + 5, True)
-
+        works(0, early)
+        hop_b(7, True)
+        works(early, 16)
         between()
         gather_last(rowp, csems).wait_recv()
 
@@ -240,10 +244,16 @@
     xrsem, zrsem = (xr_s, gp_r.at[0]), (zr_s, gp_r.at[1])
 
     def start_work():
+        for load in loads[3:]:
+            load.wait()
+        for k, ref in enumerate((idv0, idv1, idv2)):
+            idv[pl.ds(k, 1), pl.ds(0, slots)] = ref[...].reshape(1, slots)
+        move = pltpu.make_async_copy(idv, named, in_sem.at[6])
+        move.start()
+        move.wait()
         for s in range(slots):
-            ids[0, s] = left[s]
-            ids[1, s] = right[s]
-            ids[2, s] = active[s]
+            for k in range(3):
+                ids[k, s] = named[k, s]
         ids[0, slots] = c
         ids[1, slots] = r
         ids[2, slots] = 1
@@ -253,13 +263,13 @@
             def _(a):
                 packed = jnp.int32(0)
                 for s in range(slots):
-                    ident = left[s] if which == 0 else right[s]
+                    ident = named[which, s]
                     packed = jnp.where(ident == a, packed * 16 + (s + 1), packed)
                 lists[which, a] = packed
 
         packs(0, 16)
         packs(1, 8)
-        for load in loads[1:]:
+        for load in loads[1:3]:
             load.wait()
 
     def w_product(s):
@@ -343,7 +353,7 @@
                 y_ring(g, h).start()
 
     gather_phase(
-        xrow, xcol, xt, xt, xsem, xrsem, start_work, lambda q, at: None, w_product, scatter_start
+        xrow, xcol, xt, xt, xsem, xrsem, start_work, lambda q, at: None, w_product, 8, scatter_start
     )
 
     def y_products(first):
@@ -410,7 +420,7 @@
         zh[c], zl[c] = split(zrow[c])
 
     gather_phase(
-        zrow, zcol, zrow.at[c], zcol.at[r], zsem, zrsem, own_seen, seen, first_half, lambda: None
+        zrow, zcol, zrow.at[c], zcol.at[r], zsem, zrsem, own_seen, seen, first_half, 0, lambda: None
     )
 
     drain(xrow, 15, x_s)
@@ -429,7 +439,9 @@
 
     def stepped(s):
         a, b = ids[0, s], ids[1, s]
-        grad = dot(zh[a], xh[b]) + dot(zh[a], xl[b]) + dot(zl[a], xh[b])
+        za, zb = zh[a], zl[a]
+        xa, xb = xh[b], xl[b]
+        grad = dot(jnp.concatenate([za, zb, za], 1), jnp.concatenate([xb, xa, xa], 0))
         return tile[s] - scale * ids[2, s].astype(F32) * grad
 
     def out(s):
@@ -471,7 +483,7 @@
             pltpu.VMEM((rows, samp, side), BF16),
             pltpu.SMEM((3, slots + 1), jnp.int32),
         ),
-        in_specs=[anyw] * 3 + [smem] * 3,
+        in_specs=[anyw] * 6,
         out_specs=(vmem,) * 5 + (smem,),
         scratch_shapes=[
             pltpu.VMEM((samp, side), F32),
@@ -489,9 +501,14 @@
             pltpu.VMEM((2, 4, side // 2, samp), F32),
             pltpu.VMEM((2, 3, side // 2, samp), F32),
             pltpu.SMEM((2, 16), jnp.int32),
+            pltpu.VMEM((slots,), jnp.int32),
+            pltpu.VMEM((slots,), jnp.int32),
+            pltpu.VMEM((slots,), jnp.int32),
+            pltpu.VMEM((8, 128), jnp.int32),
+            pltpu.SMEM((8, 128), jnp.int32),
             dma((4, 3)), dma((4, 8)), dma(()), dma(()), dma((2, 3)), dma((2,)),
             dma((4, 3)), dma((4, 12)), dma((2, 3)), dma((2, 4)),
-            dma(()), dma(()), dma(()), dma(()), dma(()), dma(()), dma((3,)),
+            dma(()), dma(()), dma(()), dma(()), dma(()), dma(()), dma((7,)),
         ],
         compiler_params=pltpu.CompilerParams(
             collective_id=0, has_side_effects=True, vmem_limit_bytes=48 * 1024 * 1024

time: 117 us -> 114 us (0.974)
  Pallas kernels: 116 us -> 113 us
    pallas_call x1, Pallas kernels: 112 us -> 109 us  [per_device(): pl.pallas_call(kernel, out_shape=(pltpu.VMEM((slots + 1, side, side), F32...]
where the time goes in v4:
time: 114 us
  Pallas kernels  113 us (99%)
    pallas_call x1, Pallas kernels, per_device(): pl.pallas_call(kernel, out_shape=(pltpu.VMEM((slots + 1, side, side), F32...  109 us
    pallas_call x1, Pallas kernels, per_device(): pl.pallas_call(finish, out_shape=(jax.ShapeDtypeStruct((slots, side, side...  4.04 us

profile of v4, /device:TPU:1, one launch (start us, length us, event | category | flops | bytes accessed | tf_op | source)
XLA Modules:
  0.0 113.6 jit_solution(18047002240105077528)
XLA Ops:
  0.6 108.8 %shard_map.77 = (f32[16,256,256]{2,1,0:T(8,128)S(1)}, bf16[16,256,384]{2,1,0:T(8,128)(2,1)S(1)}, bf16[16,256,384]{2,1,0:T(8,128)(2,1)S(1)}, bf16[8,384,256]{2,1,...) custom-call(f32[384,256]{1,0:T(8,128)} %samples_hbm.1, f32[15,256,256]{2,1,0:T(8,128)} %bitcast.5, ...), custom_call_target="tpu_custom_call" | custom-call | tf_op jit(solution)/shard_map/pallas_call | solution.py:476
  109.4 4.0 %shard_map.78 = (f32[15,256,256]{2,1,0:T(8,128)}, f32[256,256]{1,0:T(8,128)}) custom-call(f32[16,256,256]{2,1,0:T(8,128)S(1)} %get-tuple-element.10.tile, bf16[16,256,384]{2,1,0:T(8,128)(2,1)S(1)} %get-tuple-element.11.zh, bf16[16,256,384]{2,1,0:T(8,128)(2,1)S(1)} %get-tuple-element.12.zl, bf16[8,384,256]{2,1,0:T(8,128)(2,1)S(1)} %get-tuple-element.13.xh, ...), custom_call_target="tpu_custom_call" | custom-call | tf_op jit(solution)/shard_map/pallas_call | solution.py:524

commit v5 on v4

--- a/solution.py
+++ b/solution.py
@@ -17,6 +17,22 @@
 NT = (((1,), (1,)), ((), ()))
 TN = (((0,), (0,)), ((), ()))
 ROUTES = ((True, 1), (True, -1), (False, 1), (False, -1))
+
+ORDER = (
+    "xs0", "xs1", "xa00", "xa01", "xb00", "xx00", "xx01", "xa10", "xa11", "xb01", "xb11",
+    "xx11", "xa20", "prep", "xb10", "xx10", "xb20", "xa21", "xb30", "xb21", "xb31", "xb40",
+    "xx20", "xb50", "xb60", "xb41", "xb51", "xx21", "xh", "wp0", "xb61", "xb71", "wp1", "xb70",
+    "wp2", "wp3", "w011", "w000", "w030", "w001", "w031", "w010", "xl", "yp0", "yp1", "w100",
+    "w111", "w020", "yp2", "w101", "yp3", "ye00", "w110", "w021", "ye01", "w200", "yc00",
+    "ye10", "ye20", "w211", "ye11", "yc01", "split", "w201", "w120", "w210", "yc10", "w300",
+    "w121", "yc11", "w311", "yr10", "w131", "ye30", "ye21", "w130", "yr11", "w301", "yc20",
+    "ye31", "yc30", "yc21", "w310", "yc31", "w220", "wa10", "yr20", "w221", "wa11", "yr21",
+    "w230", "w320", "wa20", "w231", "w321", "wa21", "w330", "wa30", "yr30", "zs0", "yr31",
+    "w331", "wa31", "zs1", "za00", "za01", "zb01", "za10", "zx00", "zx01", "za11", "zb00",
+    "zb11", "za20", "za21", "zx10", "zx11", "zb10", "zb21", "zb20", "zb30", "zb40", "zb31",
+    "zb41", "zx21", "zb51", "zb50", "zx20", "zh", "gp0", "gp1", "zb60", "zb61", "zb71", "gp2",
+    "zb70", "gp3", "zl",
+)
 
 
 def split(v):
@@ -157,71 +173,6 @@
         ref = panel.at[pl.ds(0, 4)]
         return remote(ref, ref, sems[0], sems[1], partner, c)
 
-    def gather_phase(rowp, colp, own_row, own_col, csems, rsems, first_work, seen, work, early, between):
-        for q in range(4):
-            gather_a(rowp, q, 0, own_row, csems).start()
-        for g in range(2):
-            ring(colp, g, 0, own_col, rsems).start()
-            hand(colp, g, 0, own_col, rsems).start()
-        for q in range(4):
-            gather_b(rowp, q, 0, own_row, csems).start()
-        first_work()
-
-        def hop_a(h):
-            for q in range(4):
-                gather_a_arrival(rowp, q, h, csems).wait_recv()
-                if h < 2:
-                    gather_a(rowp, q, h + 1, own_row, csems).start()
-            for q in range(4):
-                gather_b(rowp, q, h + 1, None, csems).start()
-            for q in range(4):
-                seen(q, col_of(q, mod4(pos_a[q] - ROUTES[q][1] * (h + 1)), pos_b[q]))
-
-        def hop_x(h):
-            for g in range(2):
-                ring_arrival(colp, g, h, rsems).wait_recv()
-                if h < 2:
-                    ring(colp, g, h + 1, own_col, rsems).start()
-                hand(colp, g, h + 1, own_col, rsems).start()
-
-        def hop_b(i, last):
-            for q in range(4):
-                gather_b_arrival(rowp, q, i, csems).wait_recv()
-                gather_b(rowp, q, i + 4, None, csems, last).start()
-            for q in range(4):
-                seen(q, arrived_b(q, i))
-
-        def works(first, last):
-            @pl.loop(first // 4, last // 4)
-            def _(i):
-                for k in range(4):
-                    work(i * 4 + k)
-
-        hop_a(0)
-        hop_b(0, False)
-        hop_a(1)
-        hop_x(0)
-        hop_b(1, False)
-        hop_a(2)
-        hop_b(2, False)
-        hop_x(1)
-        hop_b(3, False)
-        hop_b(4, True)
-        hop_b(5, True)
-        hop_x(2)
-        hop_b(6, True)
-        hand_arrivals(colp, rsems).wait_recv()
-        works(0, early)
-        hop_b(7, True)
-        works(early, 16)
-        between()
-        gather_last(rowp, csems).wait_recv()
-
-        @pl.loop(8, 12)
-        def _(i):
-            for q in range(4):
-                seen(q, arrived_b(q, i))
-
     def drain(ref, blocks, sem):
         ref = ref.at[pl.ds(0, blocks)]
         remote(ref, ref, sem, in_sem.at[0], partner, c).wait_send()
@@ -298,29 +249,6 @@
     def scatter_a_arrival(q, h):
         return remote(rsa.at[q, h], rsa.at[q, h], w_s, wa_r.at[q, h], r, next_a(q))
 
-    def scatter_start():
-        for j in range(4):
-            for q in range(4):
-                rs0[q, j] = w_sum(scatter_target(q, 0, j), qrows(q))
-            for q in range(4):
-                scatter_b0(q, j).start()
-
-    def scatter_hop(h, j):
-        i = (h - 1) * 4 + j
-        for q in range(4):
-            scatter_b_arrival(q, i).wait_recv()
-            rsb[q, i] = rsb[q, i] + w_sum(scatter_target(q, h, j), qrows(q))
-        if h < 3:
-            for q in range(4):
-                scatter_b(q, i).start()
-
-    def scatter_step(h):
-        for q in range(4):
-            scatter_a_arrival(q, h - 1).wait_recv()
-            rsa[q, h - 1] = rsa[q, h - 1] + rsb[q, 8 + h]
-        for q in range(4):
-            scatter_a(q, h).start()
-
     def y_target(g, h):
         return mod4(x - (1, -1)[g] * (h + 1))
 
@@ -331,97 +259,150 @@
         src = yx.at[g, 0] if h == 0 else yr.at[g, h - 1]
         return remote(src, yr.at[g, h], y_s, yh_r.at[g, h], next_x(g), c)
 
-    def y_exchange(h):
-        for g in range(2):
+    scale = STEP_SIZE / (2.0 * samp)
+
+    def first_half(s):
+        factor = scale * ids[2, s].astype(F32)
+        grad = dot3(xrow[ids[0, s]], zcol[ids[1, s]], NT)
+        tile[s] = tile[s] - factor * grad
+
+    def work(kind, k):
+        product = {"w": w_product, "y": y_product, "g": first_half}[kind]
+        top = slots - 1 if kind == "y" else slots
+
+        for n in range(4 * k, min(4 * k + 4, top + 1)):
+            product(n)
+
+        if kind == "w" and k == 3:
+            eye = lax.broadcasted_iota(jnp.int32, (side, side), 0) == lax.broadcasted_iota(
+                jnp.int32, (side, side), 1
+            )
+            diag = tile[slots]
+            tile[slots] = diag + jnp.where(eye, STEP_SIZE / jnp.where(eye, diag, 1.0), 0.0)
+
+    def keep(q, at):
+        zh[at, qrows(q), :], zl[at, qrows(q), :] = split(zrow[at, qrows(q), :])
+
+    def split_x():
+        @pl.loop(0, xh.shape[0])
+        def _(b):
+            xh[b], xl[b] = split(xcol[b].T)
+
+    def gather_step(p, step, i, g):
+        z = p == "z"
+        rowp, colp = (zrow, zcol) if z else (xrow, xcol)
+        own_row, own_col = (zrow.at[c], zcol.at[r]) if z else (xt, xt)
+        csems, rsems = (zsem, zrsem) if z else (xsem, xrsem)
+        routes = (2 * g, 2 * g + 1)
+        if step == "s":
+            if z:
+                for q in routes:
+                    part = pl.ds((q % 2) * quarter, quarter)
+                    total = rsa[q, 2] + rsb[q, 11] + yr[g, 2, part, :] + pw[slots + 1, qrows(q), :]
+                    zrow[c, qrows(q), :] = total
+                    zcol[r, qrows(q), :] = total
+            for q in routes:
+                gather_a(rowp, q, 0, own_row, csems).start()
+            ring(colp, g, 0, own_col, rsems).start()
+            hand(colp, g, 0, own_col, rsems).start()
+            for q in routes:
+                gather_b(rowp, q, 0, own_row, csems).start()
+            if z:
+                for q in routes:
+                    keep(q, c)
+        elif step == "a":
+            for q in routes:
+                gather_a_arrival(rowp, q, i, csems).wait_recv()
+                if i < 2:
+                    gather_a(rowp, q, i + 1, own_row, csems).start()
+            for q in routes:
+                gather_b(rowp, q, i + 1, None, csems).start()
+            if z:
+                for q in routes:
+                    keep(q, col_of(q, mod4(pos_a[q] - ROUTES[q][1] * (i + 1)), pos_b[q]))
+        elif step == "b":
+            for q in routes:
+                gather_b_arrival(rowp, q, i, csems).wait_recv()
+                gather_b(rowp, q, i + 4, None, csems, i >= 4).start()
+            if z:
+                for q in routes:
+                    keep(q, arrived_b(q, i))
+        elif step == "x":
+            ring_arrival(colp, g, i, rsems).wait_recv()
+            if i < 2:
+                ring(colp, g, i + 1, own_col, rsems).start()
+            hand(colp, g, i + 1, own_col, rsems).start()
+        elif step == "h":
+            hand_arrivals(colp, rsems).wait_recv()
+        else:
+            gather_last(rowp, csems).wait_recv()
+            if z:
+
+                @pl.loop(8, 12)
+                def _(n):
+                    for q in range(4):
+                        keep(q, arrived_b(q, n))
+
+    def scatter_step(h, j, g):
+        routes = (2 * g, 2 * g + 1)
+        i = (h - 1) * 4 + j
+        for q in routes:
+            if h == 0:
+                rs0[q, j] = w_sum(scatter_target(q, 0, j), qrows(q))
+            else:
+                scatter_b_arrival(q, i).wait_recv()
+                rsb[q, i] = rsb[q, i] + w_sum(scatter_target(q, h, j), qrows(q))
+        for q in routes:
+            if h == 0:
+                scatter_b0(q, j).start()
+            elif h < 3:
+                scatter_b(q, i).start()
+            elif j == 0:
+                scatter_a(q, 0).start()
+
+    def scatter_turn(n, g):
+        routes = (2 * g, 2 * g + 1)
+        for q in routes:
+            scatter_a_arrival(q, n - 1).wait_recv()
+            if n < 3:
+                rsa[q, n - 1] = rsa[q, n - 1] + rsb[q, 8 + n]
+        if n < 3:
+            for q in routes:
+                scatter_a(q, n).start()
+
+    def y_step(step, h, g):
+        if step == "e":
             ys[g, h] = y_sum(2 * y_target(g, h) + other, hrows(g))
-        for g in range(2):
             y_give(g, h).start()
-
-    def y_combine(h):
-        for g in range(2):
+        elif step == "c":
             y_give(g, h).wait_recv()
             yx[g, h] = yx[g, h] + y_sum(2 * y_target(g, h) + core, hrows(g))
-        if h == 0:
-            for g in range(2):
+            if h == 0:
                 y_ring(g, 0).start()
-
-    def y_hop(h):
-        for g in range(2):
+        else:
             y_ring(g, h - 1).wait_recv()
             yr[g, h - 1] = yr[g, h - 1] + yx[g, h]
             if h < 3:
                 y_ring(g, h).start()
 
-    gather_phase(
-        xrow, xcol, xt, xt, xsem, xrsem, start_work, lambda q, at: None, w_product, 8, scatter_start
-    )
-
-    def y_products(first):
-        @pl.loop(0, 4)
-        def _(k):
-            y_product(jnp.minimum(first + k, slots - 1))
-
-    for j in range(2):
-        y_products(8 * j)
-        scatter_hop(1, j)
-        y_products(8 * j + 4)
-    y_exchange(0)
-    scatter_hop(2, 0)
-    y_exchange(1)
-    scatter_hop(1, 2)
-    y_exchange(2)
-    y_combine(0)
-    scatter_hop(2, 1)
-    y_exchange(3)
-    scatter_hop(1, 3)
-    y_combine(1)
-    y_combine(2)
-    y_combine(3)
-    scatter_hop(3, 0)
-    for q in range(4):
-        scatter_a(q, 0).start()
-
-    @pl.loop(0, 8)
-    def _(b):
-        xh[b], xl[b] = split(xcol[b].T)
-
-    eye = lax.broadcasted_iota(jnp.int32, (side, side), 0) == lax.broadcasted_iota(
-        jnp.int32, (side, side), 1
-    )
-    tile[slots] = tile[slots] + jnp.where(eye, STEP_SIZE / jnp.where(eye, tile[slots], 1.0), 0.0)
-    scatter_hop(2, 2)
-    y_hop(1)
-    scatter_hop(3, 1)
-    scatter_step(1)
-    scatter_hop(2, 3)
-    y_hop(2)
-    scatter_hop(3, 2)
-    scatter_step(2)
-    scatter_hop(3, 3)
-    y_hop(3)
-    for q in range(4):
-        scatter_a_arrival(q, 2).wait_recv()
-        part = pl.ds((q % 2) * quarter, quarter)
-        total = rsa[q, 2] + rsb[q, 11] + yr[q // 2, 2, part, :] + pw[slots + 1, qrows(q), :]
-        zrow[c, qrows(q), :] = total
-        zcol[r, qrows(q), :] = total
-
-    scale = STEP_SIZE / (2.0 * samp)
-
-    def first_half(s):
-        factor = scale * ids[2, s].astype(F32)
-        grad = dot3(xrow[ids[0, s]], zcol[ids[1, s]], NT)
-        tile[s] = tile[s] - factor * grad
-
-    def seen(q, at):
-        zh[at, qrows(q), :], zl[at, qrows(q), :] = split(zrow[at, qrows(q), :])
-
-    def own_seen():
-        zh[c], zl[c] = split(zrow[c])
-
-    gather_phase(
-        zrow, zcol, zrow.at[c], zcol.at[r], zsem, zrsem, own_seen, seen, first_half, 0, lambda: None
-    )
+    for name in ORDER:
+        kind, step = name[0], name[1]
+        numbers = [int(n) for n in name[2:] if n.isdigit()]
+        if name == "prep":
+            start_work()
+        elif name == "split":
+            split_x()
+        elif step == "p":
+            work(kind, numbers[0])
+        elif kind in "xz":
+            i, g = ([0] + numbers)[-2:] if numbers else (0, 0)
+            gather_step(kind, step, i, g)
+        elif kind == "w" and step == "a":
+            scatter_turn(*numbers)
+        elif kind == "w":
+            scatter_step(int(step), *numbers)
+        else:
+            y_step(step, *numbers)
 
     drain(xrow, 15, x_s)
     drain(xcol, 7, xr_s)

time: 114 us -> 113 us (level)
  no operation moved by 1% of the time
where the time goes in v5:
time: 113 us
  Pallas kernels  112 us (99%)
    pallas_call x1, Pallas kernels, per_device(): pl.pallas_call(kernel, out_shape=(pltpu.VMEM((slots + 1, side, side), F32...  108 us
    pallas_call x1, Pallas kernels, per_device(): pl.pallas_call(finish, out_shape=(jax.ShapeDtypeStruct((slots, side, side...  4.06 us

profile of v5, /device:TPU:1, one launch (start us, length us, event | category | flops | bytes accessed | tf_op | source)
XLA Modules:
  0.0 112.6 jit_solution(15430086487027455244)
XLA Ops:
  0.6 107.7 %shard_map.77 = (f32[16,256,256]{2,1,0:T(8,128)S(1)}, bf16[16,256,384]{2,1,0:T(8,128)(2,1)S(1)}, bf16[16,256,384]{2,1,0:T(8,128)(2,1)S(1)}, bf16[8,384,256]{2,1,...) custom-call(f32[384,256]{1,0:T(8,128)} %samples_hbm.1, f32[15,256,256]{2,1,0:T(8,128)} %bitcast.5, ...), custom_call_target="tpu_custom_call" | custom-call | tf_op jit(solution)/shard_map/pallas_call | solution.py:457
  108.3 4.1 %shard_map.78 = (f32[15,256,256]{2,1,0:T(8,128)}, f32[256,256]{1,0:T(8,128)}) custom-call(f32[16,256,256]{2,1,0:T(8,128)S(1)} %get-tuple-element.10.tile, bf16[16,256,384]{2,1,0:T(8,128)(2,1)S(1)} %get-tuple-element.11.zh, bf16[16,256,384]{2,1,0:T(8,128)(2,1)S(1)} %get-tuple-element.12.zl, bf16[8,384,256]{2,1,0:T(8,128)(2,1)S(1)} %get-tuple-element.13.xh, ...), custom_call_target="tpu_custom_call" | custom-call | tf_op jit(solution)/shard_map/pallas_call | solution.py:505

commit v6 on v5

--- a/solution.py
+++ b/solution.py
@@ -19,19 +19,20 @@
 ROUTES = ((True, 1), (True, -1), (False, 1), (False, -1))
 
 ORDER = (
-    "xs0", "xs1", "xa00", "xa01", "xb00", "xx00", "xx01", "xa10", "xa11", "xb01", "xb11",
-    "xx11", "xa20", "prep", "xb10", "xx10", "xb20", "xa21", "xb30", "xb21", "xb31", "xb40",
-    "xx20", "xb50", "xb60", "xb41", "xb51", "xx21", "xh", "wp0", "xb61", "xb71", "wp1", "xb70",
-    "wp2", "wp3", "w011", "w000", "w030", "w001", "w031", "w010", "xl", "yp0", "yp1", "w100",
-    "w111", "w020", "yp2", "w101", "yp3", "ye00", "w110", "w021", "ye01", "w200", "yc00",
-    "ye10", "ye20", "w211", "ye11", "yc01", "split", "w201", "w120", "w210", "yc10", "w300",
-    "w121", "yc11", "w311", "yr10", "w131", "ye30", "ye21", "w130", "yr11", "w301", "yc20",
-    "ye31", "yc30", "yc21", "w310", "yc31", "w220", "wa10", "yr20", "w221", "wa11", "yr21",
-    "w230", "w320", "wa20", "w231", "w321", "wa21", "w330", "wa30", "yr30", "zs0", "yr31",
-    "w331", "wa31", "zs1", "za00", "za01", "zb01", "za10", "zx00", "zx01", "za11", "zb00",
-    "zb11", "za20", "za21", "zx10", "zx11", "zb10", "zb21", "zb20", "zb30", "zb40", "zb31",
-    "zb41", "zx21", "zb51", "zb50", "zx20", "zh", "gp0", "gp1", "zb60", "zb61", "zb71", "gp2",
-    "zb70", "gp3", "zl",
+    "xs0", "xs1", "xa00", "xa01", "xx01", "xa10", "xb01", "xx00", "xa11", "xb11", "xb00",
+    "prep", "xa20", "xx10", "xa21", "xx11", "xb10", "xb20", "xb21", "xb30", "xb40", "xb31",
+    "xx20", "xb41", "xb51", "xb50", "xb60", "xx21", "xh", "xb61", "wp0", "wp1", "wp2", "xb70",
+    "wp3", "wp4", "xb71", "wp5", "wp6", "wp7", "w000", "w010", "w001", "w011", "w020", "w031",
+    "xl", "yp0", "yp1", "yp2", "yp3", "w100", "w101", "w030", "yp4", "w021", "yp5", "w110",
+    "w111", "yp6", "yp7", "ye00", "ye10", "ye01", "yc00", "w200", "yc01", "w201", "w121",
+    "w120", "ye20", "yc10", "ye11", "ye21", "ye30", "ye31", "w210", "yc11", "w300", "w301",
+    "yr10", "w211", "w220", "yr11", "w221", "w310", "wa10", "yc21", "w130", "yc31", "w311",
+    "yc20", "wa11", "w131", "w320", "yr20", "yr21", "w230", "w321", "wa20", "w231", "wa21",
+    "yc30", "yr30", "w330", "wa30", "zs0", "yr31", "split", "w331", "wa31", "zs1", "za00",
+    "za01", "zx00", "zb01", "za10", "zx01", "za11", "zb11", "zb00", "za20", "zx11", "za21",
+    "zx10", "zb10", "zb20", "zb21", "zb30", "zb31", "zx20", "zb41", "zx21", "zb40", "zb51",
+    "zb50", "zh", "zb60", "gp0", "zb70", "zb61", "zb71", "gp1", "gp2", "gp3", "gp4", "gp5",
+    "gp6", "gp7", "zl",
 )
 
 
@@ -115,12 +116,7 @@
     for load in loads:
         load.start()
     loads[0].wait()
-    own = raw[...].T
-    xt[...] = own
-    xrow[c] = own
-    xcol[r] = own
-    pw[0] = jnp.zeros((side, samp), F32)
-    py[0] = jnp.zeros((side, samp), F32)
+    xt[...] = raw[...].T
     pl.semaphore_wait(barrier, len(peers))
 
     def gather_a(panel, q, h, own, sems):
@@ -195,6 +191,10 @@
     xrsem, zrsem = (xr_s, gp_r.at[0]), (zr_s, gp_r.at[1])
 
     def start_work():
+        xrow[c] = xt[...]
+        xcol[r] = xt[...]
+        pw[0] = jnp.zeros((side, samp), F32)
+        py[0] = jnp.zeros((side, samp), F32)
         for load in loads[3:]:
             load.wait()
         for k, ref in enumerate((idv0, idv1, idv2)):
@@ -270,10 +270,9 @@
         product = {"w": w_product, "y": y_product, "g": first_half}[kind]
         top = slots - 1 if kind == "y" else slots
 
-        for n in range(4 * k, min(4 * k + 4, top + 1)):
+        for n in range(2 * k, min(2 * k + 2, top + 1)):
             product(n)
-
-        if kind == "w" and k == 3:
+        if kind == "w" and 2 * k + 1 >= slots:
             eye = lax.broadcasted_iota(jnp.int32, (side, side), 0) == lax.broadcasted_iota(
                 jnp.int32, (side, side), 1
             )

time: 113 us -> 112 us (level)
    pallas_call x1, Pallas kernels: 108 us -> 107 us  [per_device(): pl.pallas_call(kernel, out_shape=(pltpu.VMEM((slots + 1, side, side), F32...]
where the time goes in v6:
time: 112 us; the launch traced here: 111 us
  Pallas kernels  111 us (99%)
    pallas_call x1, Pallas kernels, per_device(): pl.pallas_call(kernel, out_shape=(pltpu.VMEM((slots + 1, side, side), F32...  107 us
    pallas_call x1, Pallas kernels, per_device(): pl.pallas_call(finish, out_shape=(jax.ShapeDtypeStruct((slots, side, side...  4.05 us

profile of v6, /device:TPU:1, one launch (start us, length us, event | category | flops | bytes accessed | tf_op | source)
XLA Modules:
  0.0 111.4 jit_solution(13875015366813946073)
XLA Ops:
  0.6 106.5 %shard_map.77 = (f32[16,256,256]{2,1,0:T(8,128)S(1)}, bf16[16,256,384]{2,1,0:T(8,128)(2,1)S(1)}, bf16[16,256,384]{2,1,0:T(8,128)(2,1)S(1)}, bf16[8,384,256]{2,1,...) custom-call(f32[384,256]{1,0:T(8,128)} %samples_hbm.1, f32[15,256,256]{2,1,0:T(8,128)} %bitcast.5, ...), custom_call_target="tpu_custom_call" | custom-call | tf_op jit(solution)/shard_map/pallas_call | solution.py:456
  107.2 4.0 %shard_map.78 = (f32[15,256,256]{2,1,0:T(8,128)}, f32[256,256]{1,0:T(8,128)}) custom-call(f32[16,256,256]{2,1,0:T(8,128)S(1)} %get-tuple-element.10.tile, bf16[16,256,384]{2,1,0:T(8,128)(2,1)S(1)} %get-tuple-element.11.zh, bf16[16,256,384]{2,1,0:T(8,128)(2,1)S(1)} %get-tuple-element.12.zl, bf16[8,384,256]{2,1,0:T(8,128)(2,1)S(1)} %get-tuple-element.13.xh, ...), custom_call_target="tpu_custom_call" | custom-call | tf_op jit(solution)/shard_map/pallas_call | solution.py:504

commit v7 on v6

--- a/solution.py
+++ b/solution.py
@@ -46,7 +46,8 @@
     ah, al = split(a)
     bh, bl = split(b)
     dot = functools.partial(lax.dot_general, dimension_numbers=dims, preferred_element_type=F32)
-    return dot(ah, bh) + dot(ah, bl) + dot(al, bh)
+    ka, kb = dims[0][0][0], dims[0][1][0]
+    return dot(jnp.concatenate([ah, al, ah], ka), jnp.concatenate([bl, bh, bh], kb))
 
 
 def mod4(v):

time: 112 us -> 112 us (level)
  no operation moved by 1% of the time
where the time goes in v7:
time: 112 us; the launch traced here: 111 us
  Pallas kernels  111 us (99%)
    pallas_call x1, Pallas kernels, per_device(): pl.pallas_call(kernel, out_shape=(pltpu.VMEM((slots + 1, side, side), F32...  106 us
    pallas_call x1, Pallas kernels, per_device(): pl.pallas_call(finish, out_shape=(jax.ShapeDtypeStruct((slots, side, side...  4.05 us

profile of v7, /device:TPU:1, one launch (start us, length us, event | category | flops | bytes accessed | tf_op | source)
XLA Modules:
  0.0 111.3 jit_solution(15119093890664538399)
XLA Ops:
  0.6 106.5 %shard_map.77 = (f32[16,256,256]{2,1,0:T(8,128)S(1)}, bf16[16,256,384]{2,1,0:T(8,128)(2,1)S(1)}, bf16[16,256,384]{2,1,0:T(8,128)(2,1)S(1)}, bf16[8,384,256]{2,1,...) custom-call(f32[384,256]{1,0:T(8,128)} %samples_hbm.1, f32[15,256,256]{2,1,0:T(8,128)} %bitcast.5, ...), custom_call_target="tpu_custom_call" | custom-call | tf_op jit(solution)/shard_map/pallas_call | solution.py:457
  107.1 4.0 %shard_map.78 = (f32[15,256,256]{2,1,0:T(8,128)}, f32[256,256]{1,0:T(8,128)}) custom-call(f32[16,256,256]{2,1,0:T(8,128)S(1)} %get-tuple-element.10.tile, bf16[16,256,384]{2,1,0:T(8,128)(2,1)S(1)} %get-tuple-element.11.zh, bf16[16,256,384]{2,1,0:T(8,128)(2,1)S(1)} %get-tuple-element.12.zl, bf16[8,384,256]{2,1,0:T(8,128)(2,1)S(1)} %get-tuple-element.13.xh, ...), custom_call_target="tpu_custom_call" | custom-call | tf_op jit(solution)/shard_map/pallas_call | solution.py:505
